TPU v7x, 32 devices: a whole 2x2x4 slice. The times are simulated.
32 devices in a mesh: cell: 2 (over x), ap: 8 (over z, y), sc: 2 (over core).
Axes of the slice: x: 2, y: 2, z: 4, core: 2. Of those that a mesh axis runs over, the one named last changes fastest.
Arguments:
- unsmoothed_link_guesses: bfloat16 [32, 4, 2, 128, 2048], P(('cell', 'ap'), None, None, None, 'sc'), parts along dimension 0, may hold values from -24 to 24
- received: bfloat16 [32, 4, 2, 4, 2048], P(('cell', 'ap'), None, None, None, 'sc'), parts along dimension 0, may hold values from -6 to 6
- user_power: float32 [256], P('cell'), parts along dimension 0, may hold values from 0.25 to 4
- noise_power: float32 [32], P(('cell', 'ap')), parts along dimension 0, may hold values from 0.1 to 1
- ap_gain: float32 [32, 128], P(('cell', 'ap')), parts along dimension 0, may hold values from 0.5 to 4
- user_cluster: int32 [256], P('cell'), parts along dimension 0, may hold values from 0 to 15, as said below
- serving: int32 [32, 16], P('cell'), parts along dimension 0, may hold values from 0 to 1, as said below
- cluster_owner: int32 [32, 1], P('cell'), parts along dimension 0, may hold values from 0 to 7, as said below
Outputs:
- estimates: float32 [64, 8, 4, 2, 2048], P(('cell', 'ap'), None, None, None, 'sc'), parts along dimension 0
There are 2 independent parts, one for each index of `cell`. A program takes and returns all parts, laid end to end along the dimension named above; each array names one. Nothing has to cross between parts.
Inputs may be any that keep to these rules, and one draw needn't show every extreme that they name: `user_cluster`: each of the 16 clusters holds exactly 8 users. `serving`: column a belongs to index a // 2 of ap. Where a cluster is served by an index of ap, at least one of its access points serves it. Of the clusters that one index of ap serves, at most 2 have the same owner; in every draw some owner has exactly 2 of its clusters served by every index of ap. `cluster_owner`: at most 4 clusters have the same owner, and some owner has exactly 4.
All inputs are finite; a program needn't handle non-finite values.
Results may differ from a plain program's by a relative error of at most 0.017.
Values may be sent and summed in bfloat16 or wider, within the bound.
A program may use at most 128 MiB of HBM per device.

v0:
```python
import math

import jax
import jax.numpy as jnp
from jax import lax
from jax.sharding import PartitionSpec as P

TONE_NUMBER = 2048
TAPS = 64
CU = 8
OWN_MAX = 4


def complex_times(left_factor, right_factor):
    return (
        left_factor[0] * right_factor[0] - left_factor[1] * right_factor[1],
        left_factor[0] * right_factor[1] + left_factor[1] * right_factor[0],
    )


def times_conj(left_factor, right_factor):
    return (
        left_factor[0] * right_factor[0] + left_factor[1] * right_factor[1],
        left_factor[1] * right_factor[0] - left_factor[0] * right_factor[1],
    )


def hermitian_solve(cov_re, cov_im, right_re, right_im):
    dimension = len(cov_re)
    factor = {}
    pivots = []
    for j in range(dimension):
        pivot_root = cov_re[j][j]
        for k in range(j):
            element = factor[j, k]
            pivot_root = pivot_root - (element[0] * element[0] + element[1] * element[1])
        pivot_root = jnp.sqrt(pivot_root)
        pivots.append(pivot_root)
        for i in range(j + 1, dimension):
            running = (cov_re[i][j], cov_im[i][j])
            for k in range(j):
                product = times_conj(factor[i, k], factor[j, k])
                running = (running[0] - product[0], running[1] - product[1])
            factor[i, j] = (running[0] / pivot_root, running[1] / pivot_root)
    forward = []
    for i in range(dimension):
        running = (right_re[i], right_im[i])
        for k in range(i):
            product = complex_times(factor[i, k], forward[k])
            running = (running[0] - product[0], running[1] - product[1])
        forward.append((running[0] / pivots[i], running[1] / pivots[i]))
    result = [None] * dimension
    for i in range(dimension - 1, -1, -1):
        running = forward[i]
        for k in range(i + 1, dimension):
            product = times_conj(result[k], factor[k, i])
            running = (running[0] - product[0], running[1] - product[1])
        result[i] = (running[0] / pivots[i], running[1] / pivots[i])
    return result


def tone_angles(lowest_tone, tone_quantity, tones_first):
    if tones_first:
        tone_values = lowest_tone + lax.broadcasted_iota(jnp.int32, (tone_quantity, TAPS), 0)
        lag_values = lax.broadcasted_iota(jnp.int32, (tone_quantity, TAPS), 1)
    else:
        tone_values = lowest_tone + lax.broadcasted_iota(jnp.int32, (TAPS, tone_quantity), 1)
        lag_values = lax.broadcasted_iota(jnp.int32, (TAPS, tone_quantity), 0)
    rotation = tone_values * lag_values % TONE_NUMBER
    return rotation.astype(jnp.float32) * (2.0 * math.pi / TONE_NUMBER)


def forward_table(lowest_tone, tone_quantity):
    angles = tone_angles(lowest_tone, tone_quantity, True)
    return jnp.concatenate([jnp.cos(angles), jnp.sin(angles)], axis=1).astype(jnp.bfloat16)


def rebuild_tables(lowest_tone, tone_quantity):
    angles = tone_angles(lowest_tone, tone_quantity, False)
    cosine = jnp.cos(angles).astype(jnp.bfloat16)
    sine = jnp.sin(angles).astype(jnp.bfloat16)
    return (jnp.concatenate([cosine, sine], axis=0), jnp.concatenate([-sine, cosine], axis=0))


def rotate_matrix():
    rows = lax.broadcasted_iota(jnp.int32, (2 * TAPS, 2 * TAPS), 0)
    cols = lax.broadcasted_iota(jnp.int32, (2 * TAPS, 2 * TAPS), 1)
    lower = jnp.where((cols < TAPS) & (rows == cols + TAPS), -1.0, 0.0)
    upper = jnp.where((cols >= TAPS) & (rows == cols - TAPS), 1.0, 0.0)
    return (lower + upper).astype(jnp.float32)


def local_estimates(smooth_re, smooth_im, power_row, noise_level, right_side, weight_row):
    antennas = smooth_re.shape[0]
    user_scale = (power_row / smooth_re.shape[1])[:, None]
    scaled_re = [smooth_re[i] * user_scale for i in range(antennas)]
    scaled_im = [smooth_im[i] * user_scale for i in range(antennas)]
    cov_re = [[None] * antennas for i in range(antennas)]
    cov_im = [[None] * antennas for i in range(antennas)]
    for i in range(antennas):
        for j in range(i + 1):
            cov_re[i][j] = jnp.sum(
                scaled_re[i] * smooth_re[j] + scaled_im[i] * smooth_im[j], axis=0
            )
            if i == j:
                cov_re[i][j] = cov_re[i][j] + noise_level
            else:
                cov_im[i][j] = jnp.sum(
                    scaled_im[i] * smooth_re[j] - scaled_re[i] * smooth_im[j], axis=0
                )
    signal = right_side.astype(jnp.float32)
    solved = hermitian_solve(cov_re, cov_im, signal[:, 0], signal[:, 1])
    est_re = (
        smooth_re[0][:, None, :] * solved[0][0][None]
        + smooth_im[0][:, None, :] * solved[0][1][None]
    )
    est_im = (
        smooth_re[0][:, None, :] * solved[0][1][None]
        - smooth_im[0][:, None, :] * solved[0][0][None]
    )
    for i in range(1, antennas):
        est_re = (
            est_re
            + smooth_re[i][:, None, :] * solved[i][0][None]
            + smooth_im[i][:, None, :] * solved[i][1][None]
        )
        est_im = (
            est_im
            + smooth_re[i][:, None, :] * solved[i][1][None]
            - smooth_im[i][:, None, :] * solved[i][0][None]
        )
    return weight_row[:, None, None, None] * jnp.stack([est_re, est_im], axis=2)


def local(
    unsmoothed_link_guesses,
    received,
    user_power,
    noise_power,
    ap_gain,
    user_cluster,
    serving,
    cluster_owner,
):
    ap_count = unsmoothed_link_guesses.shape[0]
    antennas = unsmoothed_link_guesses.shape[1]
    user_count = unsmoothed_link_guesses.shape[3]
    tone_positions = unsmoothed_link_guesses.shape[4]
    clusters = serving.shape[0]
    devices = lax.axis_size("ap")
    device = lax.axis_index("ap")
    lowest_tone = lax.axis_index("sc") * tone_positions
    products = jnp.dot(
        unsmoothed_link_guesses.reshape(-1, tone_positions),
        forward_table(lowest_tone, tone_positions),
        preferred_element_type=jnp.float32,
    )
    products = products.reshape((ap_count, antennas, 2, user_count, 2 * TAPS))
    rotated = jnp.dot(
        products[:, :, 1].reshape(-1, 2 * TAPS), rotate_matrix(), precision=lax.Precision.HIGHEST
    )
    combined = (
        products[:, :, 0] + rotated.reshape((ap_count, antennas, user_count, 2 * TAPS))
    ) / TONE_NUMBER
    coefficients = lax.psum(combined.astype(jnp.bfloat16), "sc")
    coef_b = coefficients.reshape(-1, 2 * TAPS)
    table_re, table_im = rebuild_tables(lowest_tone, tone_positions)
    smooth_re = jnp.dot(coef_b, table_re, preferred_element_type=jnp.float32).reshape(
        (ap_count, antennas, user_count, tone_positions)
    )
    smooth_im = jnp.dot(coef_b, table_im, preferred_element_type=jnp.float32).reshape(
        (ap_count, antennas, user_count, tone_positions)
    )
    cluster_ids = jnp.arange(clusters, dtype=jnp.int32)
    onehot = (user_cluster[:, None] == cluster_ids[None, :]).astype(jnp.float32)
    own_columns = lax.dynamic_slice_in_dim(serving, device * ap_count, ap_count, 1).astype(
        jnp.float32
    )
    weights = jnp.dot(onehot, own_columns, precision=lax.Precision.HIGHEST).T * ap_gain
    totals = lax.psum(jnp.sum(weights, axis=0), "ap")
    partial_value = local_estimates(
        smooth_re[0], smooth_im[0], user_power, noise_power[0], received[0], weights[0]
    )
    partial_value = partial_value + local_estimates(
        smooth_re[1], smooth_im[1], user_power, noise_power[1], received[1], weights[1]
    )
    partial_value = partial_value.astype(jnp.bfloat16)
    owner_map = cluster_owner[:, 0]
    same_owner = owner_map[:, None] == owner_map[None, :]
    earlier = cluster_ids[None, :] < cluster_ids[:, None]
    cluster_rank = jnp.sum(same_owner & earlier, axis=1)
    user_ids = jnp.arange(user_count, dtype=jnp.int32)
    position = jnp.sum(
        (user_cluster[:, None] == user_cluster[None, :]) & (user_ids[None, :] < user_ids[:, None]),
        axis=1,
    )
    member_hits = (user_cluster[None, None, :] == cluster_ids[:, None, None]) & (
        position[None, None, :] == jnp.arange(CU, dtype=jnp.int32)[None, :, None]
    )
    members = jnp.sum(jnp.where(member_hits, user_ids[None, None, :], 0), axis=2)
    slot_ids = jnp.arange(devices * OWN_MAX, dtype=jnp.int32)
    slot_hits = (owner_map[None, :] == (slot_ids // OWN_MAX)[:, None]) & (
        cluster_rank[None, :] == (slot_ids % OWN_MAX)[:, None]
    )
    hit_table = slot_hits.astype(jnp.int32)
    filled = jnp.sum(hit_table, axis=1)
    member_rows = jnp.sum(hit_table[:, :, None] * members[None], axis=1)
    picked = jnp.take(partial_value, member_rows.reshape(-1), axis=0)
    picked = picked.reshape(member_rows.shape + partial_value.shape[1:])
    owner_sums = lax.psum_scatter(
        picked * filled.astype(jnp.bfloat16)[:, None, None, None, None],
        "ap",
        scatter_dimension=0,
        tiled=True,
    ).astype(jnp.float32)
    my_hits = (
        (owner_map[None, :] == device)
        & (cluster_rank[None, :] == jnp.arange(OWN_MAX, dtype=jnp.int32)[:, None])
    ).astype(jnp.int32)
    my_rows = jnp.sum(my_hits[:, :, None] * members[None], axis=1)
    my_filled = jnp.sum(my_hits, axis=1).astype(jnp.float32)
    denominator = (
        1.0 + jnp.take(totals, my_rows.reshape(-1)).reshape(my_rows.shape) * my_filled[:, None]
    )
    return owner_sums / denominator[:, :, None, None, None]


def solution(mesh):
    placed = (
        P(("cell", "ap"), None, None, None, "sc"),
        P(("cell", "ap"), None, None, None, "sc"),
        P("cell"),
        P(("cell", "ap")),
        P(("cell", "ap"), None),
        P("cell"),
        P("cell", None),
        P("cell", None),
    )
    return jax.shard_map(
        local,
        mesh=mesh,
        in_specs=placed,
        out_specs=P(("cell", "ap"), None, None, None, "sc"),
        check_vma=False,
    )
```

profile of v0, /device:TPU:0, one launch (start us, length us, event | category | flops | bytes accessed | tf_op | source)
XLA Modules:
  0.0 179.8 jit_solution(7883190322390066773)
XLA Ops:
  6.6 2.5 %cosine_convert_fusion = (bf16[1024,64]{1,0:T(8,128)(2,1)S(1)}, bf16[1024,64]{1,0:T(8,128)(2,1)S(1)}) fusion(s32[1024]{0:T(1024)S(1)} %iota_add_fusion), kind=kLoop, calls=%fused_computation.154 | loop fusion | flops 1048576 | bytes 266240 | tf_op jit(solution)/shard_map/convert.2
  9.1 3.9 %convolution_bitcast_fusion = f32[2048,128]{0,1:T(8,128)S(1)} fusion(bf16[2048,1024]{1,0:T(8,128)(2,1)} %bitcast.232, bf16[1024,64]{1,0:T(8,128)(2,1)S(1)} %get-tuple-element.144, bf16[1024,64]{1,0:T(8,128)(2,1)S(1)} %get-tuple-element.143), kind=kOutput, calls=%fused_computation.8 | convolution fusion | flops 537395200 | bytes 5505024 | tf_op jit(solution)/shard_map/dot_general | solution.py:153
  13.0 0.9 reshape.10782
  13.9 0.8 fusion.186
  14.8 0.4 copy.34
  15.2 0.4 copy.35
  15.6 1.3 fusion.4
  16.9 0.2 reduce-scatter.2.cloned.1.call-start
  17.1 1.1 sine_convert_fusion.1
  18.2 1.0 fusion.110
  19.2 0.2 convert_reduce_fusion
  19.4 0.2 convert_reduce_fusion.1
  19.6 0.4 select_reduce_fusion
  20.2 0.1 fusion.156
  20.3 0.6 fusion.187
  21.0 0.2 fusion.188
  21.3 0.1 reshape.10784
  21.4 0.1 copy.25
  21.6 16.4 %all-reduce.2.cloned.1.call-done = bf16[1024,128]{1,0:T(8,128)(2,1)} async-done(((bf16[1024,128]{1,0:T(8,128)(2,1)}), bf16[1024,128]{1,0:T(8,128)(2,1)}) %all-reduce.2.cloned.1.call-update) | async-done | bytes 262160 | tf_op jit(solution)/shard_map/psum | solution.py:165
  38.0 1.7 fusion.82
  39.7 0.7 fusion.86
  40.4 1.1 fusion.50
  41.6 0.9 fusion.28
  42.4 0.9 fusion.24
  43.3 0.9 fusion.22
  44.2 1.0 fusion.32
  45.2 0.8 fusion.48
  46.0 0.6 rsqrt_multiply_fusion.5
  46.6 0.6 rsqrt_multiply_fusion.1
  47.3 0.6 sqrt_multiply_fusion
  48.0 0.7 rsqrt_multiply_fusion.9
  48.6 0.7 rsqrt_multiply_fusion.3
  49.3 0.7 sqrt_multiply_fusion.1
  50.0 0.1 subtract_divide_fusion.1
  50.2 0.1 subtract_divide_fusion.7
  50.4 4.1 %multiply_add_fusion = (f32[128,4,1,1024]{3,1,2,0:T(4,128)S(1)}, f32[128,4,1,1024]{3,1,2,0:T(4,128)S(1)}) fusion(f32[4,1024]{1,0:T(4,128)S(1)} %get-tuple-element.42, f32[128,1024]{1,0:T(8,128)S(1)} %get-tuple-element.103, f32[4,1024]{1,0:T(4,128)S(1)} %get-tuple-element.41, f32[128,1024]{1,0:T(8,128)S(1)} %get-tuple-element.109, ...), kind=kLoop, calls=%fused_computation.10 | loop fusion | flops 15728640 | bytes 8519680 | tf_op jit(solution)/shard_map/add | solution.py:123
  54.6 4.2 %multiply_add_fusion.1 = (f32[128,4,1,1024]{3,1,2,0:T(4,128)S(1)}, f32[128,4,1,1024]{3,1,2,0:T(4,128)S(1)}) fusion(f32[4,1024]{1,0:T(4,128)S(1)} %get-tuple-element.71, f32[128,1024]{1,0:T(8,128)S(1)} %get-tuple-element.112, f32[4,1024]{1,0:T(4,128)S(1)} %get-tuple-element.70, f32[128,1024]{1,0:T(8,128)S(1)} %get-tuple-element.114, ...), kind=kLoop, calls=%fused_computation.12 | loop fusion | flops 15728640 | bytes 8519680 | tf_op jit(solution)/shard_map/add | solution.py:123
  58.7 2.1 %fusion.1 = bf16[128,4,2,1024]{3,1,2,0:T(4,128)(2,1)S(1)} fusion(f32[128,4,1,1024]{3,1,2,0:T(4,128)S(1)} %get-tuple-element.98, f32[128,4,1,1024]{3,1,2,0:T(4,128)S(1)} %get-tuple-element.97, f32[128,4,1,1024]{3,1,2,0:T(4,128)S(1)} %get-tuple-element.96, f32[128,4,1,1024]{3,1,2,0:T(4,128)S(1)} %get-tuple-element.95, f32[128]{0:T(128)S(1)} %get-tuple-element.146, ...), kind=kLoop, calls=%fused_computation.4 | loop fusion | flops 6291456 | bytes 10486784 | tf_op jit(solution)/shard_map/convert_element_type | solution.py:187
  60.8 9.8 %gather_fusion = bf16[256,4,2,1024]{3,1,2,0:T(4,128)(2,1)} fusion(bf16[128,4,2,1024]{3,1,2,0:T(4,128)(2,1)S(1)} %fusion.1, s32[1024]{0:T(1024)S(1)} %pad_clamp_fusion.1), kind=kCustom, calls=%fused_computation | custom fusion | bytes 8389632 | tf_op jit(solution)/shard_map/jit(_take)/gather | solution.py:208
  70.7 7.1 %fusion.2 = bf16[32,8,4,2,1024]{4,1,0,3,2:T(8,128)(2,1)S(1)} fusion(bf16[256,4,2,1024]{3,1,2,0:T(4,128)(2,1)} %gather_fusion, pred[32,8]{1,0:T(8,128)(4,1)S(1)} %copy.25, bf16[32]{0:T(256)(128)(2,1)S(1)} %convert_element_type.86), kind=kLoop, calls=%fused_computation.7 | loop fusion | flops 4194304 | bytes 8388928 | tf_op jit(solution)/shard_map/mul | solution.py:211
  77.7 2.4 %copy.30 = bf16[32,8,4,2,1024]{4,1,3,2,0:T(8,128)(2,1)} copy(bf16[32,8,4,2,1024]{4,1,0,3,2:T(8,128)(2,1)S(1)} %fusion.2) | data formatting | bytes 8388608 | tf_op jit(solution)/shard_map/mul | solution.py:211
  80.3 0.1 multiply_reduce_fusion.1
  80.5 22.0 %psum.15 = f32[128]{0:T(128)S(1)} all-reduce(f32[128]{0:T(128)S(1)} %get-tuple-element.149), channel_id=1, replica_groups=mesh['cell'=2,'ap'=8,'sc'=2] {'ap'}, use_global_device_ids=true, to_apply=%region_41.42 | all-reduce | flops 128 | bytes 1024 | tf_op jit(solution)/shard_map/psum | solution.py:180
  102.5 0.7 gather_fusion.1
  103.3 0.1 fusion.177
  103.5 66.5 %reduce-scatter.2.cloned.1.call-done = bf16[4,8,4,2,1024]{4,1,3,2,0:T(8,128)(2,1)} async-done(((bf16[32,8,4,2,1024]{4,1,3,2,0:T(8,128)(2,1)}), bf16[4,8,4,2,1024]{4,1,3,2,0:T(8,128)(2,1)}) %reduce-scatter.2.cloned.1.call-update) | async-done | bytes 524304 | tf_op jit(solution)/shard_map/reduce_scatter | solution.py:210
  169.9 1.2 convert_divide_fusion
  171.2 1.8 copy.32
  (52 shorter events, 1.0 us)
Async XLA Ops:
  6.5 31.5 %all-reduce.2.cloned.1.call-start = ((), (), s32[]{:S(2)}) async-start(), calls=%async_computation.1 | async-start | bytes 524288 | tf_op jit(solution)/shard_map/psum | solution.py:165
  14.7 4.5 %copy-start.4 = (s32[128]{0:T(128)S(1)}, s32[128]{0:T(128)}, u32[]{:S(2)}) copy-start(s32[128]{0:T(128)} %param.13) | copy-start | bytes 1540
  14.7 4.7 %copy-start.2 = (s32[16,1]{0,1:T(1,128)S(1)}, s32[16,1]{0,1:T(1,128)}, u32[]{:S(2)}) copy-start(s32[16,1]{0,1:T(1,128)} %param.15) | copy-start | bytes 196
  14.7 5.6 %copy-start.7 = (f32[128]{0:T(128)S(1)}, f32[128]{0:T(128)}, u32[]{:S(2)}) copy-start(f32[128]{0:T(128)} %param.10) | copy-start | bytes 1540
  14.7 5.6 %copy-start.3 = (f32[2]{0:T(128)S(1)}, f32[2]{0:T(128)}, u32[]{:S(2)}) copy-start(f32[2]{0:T(128)} %param.11) | copy-start | bytes 28
  14.7 6.3 %copy-start.5 = (s32[16,16]{1,0:T(8,128)S(1)}, s32[16,16]{1,0:T(8,128)}, u32[]{:S(2)}) copy-start(s32[16,16]{1,0:T(8,128)} %param.14) | copy-start | bytes 3076
  14.7 6.3 %copy-start.6 = (f32[2,128]{1,0:T(2,128)S(1)}, f32[2,128]{1,0:T(2,128)}, u32[]{:S(2)}) copy-start(f32[2,128]{1,0:T(2,128)} %param.12) | copy-start | bytes 3076
  14.8 6.8 %copy-start.1 = (bf16[2,4,2,4,1024]{4,3,2,1,0:T(4,128)(2,1)S(1)}, bf16[2,4,2,4,1024]{4,3,2,1,0:T(4,128)(2,1)}, u32[]{:S(2)}) copy-start(bf16[2,4,2,4,1024]{4,3,2,1,0:T(4,128)(2,1)} %param.9) | copy-start | bytes 393220
  16.9 153.1 %reduce-scatter.2.cloned.1.call-start = ((), (), s32[]{:S(2)}) async-start(), calls=%async_computation.2 | async-start | bytes 4718592 | tf_op jit(solution)/shard_map/reduce_scatter | solution.py:210
  38.0 1.7 copy-start
Sparse Core Ops, SparseCore 0:
  17.0 20.9 all-reduce.1
  80.3 89.6 reduce-scatter.1
where the time goes:
time: 180 us
  waiting for transfers between devices  82.9 us (46%)
  other arithmetic  34.6 us (19%)
  blocking collectives  22 us (12%)
  local copies, waits for them, and re-layouts  18.4 us (10%)
  between operations  13.8 us (8%)
  matrix products  7.85 us (4%)
    reduce_scatter x1, waiting for transfers between devices, local(): lax.psum_scatter(picked * filled.astype(jnp.bfloat16)[:, None, None, None...  66.5 us
    psum x1, blocking collectives, local(): totals = lax.psum(jnp.sum(weights, axis=0), 'ap')  22 us
    psum x1, waiting for transfers between devices, local(): coefficients = lax.psum(combined.astype(jnp.bfloat16), 'sc')  16.4 us
    gather x1, local copies, waits for them, and re-layouts, local(): picked = jnp.take(partial_value, member_rows.reshape(-1), axis=0)  9.81 us
    add x2, other arithmetic, local_estimates(): est_re + smooth_re[i][:, None, :] * solved[i][0][None]  8.3 us
    mul x1, other arithmetic, local(): picked * filled.astype(jnp.bfloat16)[:, None, None, None, None]  7.08 us
    dot_general x1, matrix products, local(): jnp.dot(unsmoothed_link_guesses.reshape(-1, tone_positions), forward_tabl...  3.9 us
    another operation x3, other arithmetic  3.78 us
  transfers between devices with their start and end apart: 2, of which 2 were waited for; matrix products, arithmetic and copies ran while one was open for 3% of the time, Pallas kernels for 0%

commit v1 on v0

v1 whole, which is shorter than its diff:
```python
import functools
import math

import jax
import jax.numpy as jnp
import numpy as np
from jax import lax
from jax.experimental import pallas as pl
from jax.experimental.pallas import tpu as pltpu
from jax.sharding import PartitionSpec as P

TONE_NUMBER = 2048
TAPS = 64
CU = 8
OWN_MAX = 4
PEER_MAX = 2
MESH = pl.DeviceIdType.MESH
LANES = 128


def complex_times(left_factor, right_factor):
    return (
        left_factor[0] * right_factor[0] - left_factor[1] * right_factor[1],
        left_factor[0] * right_factor[1] + left_factor[1] * right_factor[0],
    )


def times_conj(left_factor, right_factor):
    return (
        left_factor[0] * right_factor[0] + left_factor[1] * right_factor[1],
        left_factor[1] * right_factor[0] - left_factor[0] * right_factor[1],
    )


def hermitian_solve(cov_re, cov_im, right):
    dimension = len(cov_re)
    factor = {}
    inverses = []
    for j in range(dimension):
        pivot = cov_re[j][j]
        for k in range(j):
            element = factor[j, k]
            pivot = pivot - (element[0] * element[0] + element[1] * element[1])
        inverse = 1.0 / jnp.sqrt(pivot)
        inverses.append(inverse)
        for i in range(j + 1, dimension):
            running = (cov_re[i][j], cov_im[i][j])
            for k in range(j):
                product = times_conj(factor[i, k], factor[j, k])
                running = (running[0] - product[0], running[1] - product[1])
            factor[i, j] = (running[0] * inverse, running[1] * inverse)
    forward = []
    for i in range(dimension):
        running = right[i]
        for k in range(i):
            product = complex_times(factor[i, k], forward[k])
            running = (running[0] - product[0], running[1] - product[1])
        forward.append((running[0] * inverses[i], running[1] * inverses[i]))
    result = [None] * dimension
    for i in range(dimension - 1, -1, -1):
        running = forward[i]
        for k in range(i + 1, dimension):
            product = times_conj(result[k], factor[k, i])
            running = (running[0] - product[0], running[1] - product[1])
        result[i] = (running[0] * inverses[i], running[1] * inverses[i])
    return result


def delay_tables(parts, tones):
    made = []
    for part in range(parts):
        values = part * tones + np.arange(tones, dtype=np.int32)
        rotation = np.arange(TAPS, dtype=np.int32)[:, None] * values[None, :] % TONE_NUMBER
        angles = rotation.astype(np.float32) * np.float32(2.0 * math.pi / TONE_NUMBER)
        cosine, sine = np.cos(angles), np.sin(angles)
        made.append(
            np.concatenate(
                [
                    np.concatenate([cosine, sine], axis=0),
                    np.concatenate([-sine, cosine], axis=0),
                ],
                axis=1,
            )
        )
    return np.stack(made).astype(jnp.bfloat16)


def exact_dot(left, right, dims):
    return lax.dot_general(
        left.astype(jnp.bfloat16),
        right.astype(jnp.bfloat16),
        (dims, ((), ())),
        preferred_element_type=jnp.float32,
    )


def iota(shape, dim):
    return lax.broadcasted_iota(jnp.int32, shape, dim).astype(jnp.float32)


def user_tables(user_cluster, serving, owner, clusters, users, group, n):
    onehot = (iota((clusters, users), 0) == user_cluster.astype(jnp.float32)).astype(jnp.float32)
    owner_col = owner.astype(jnp.float32)
    square = (clusters, clusters)
    rows, cols = iota(square, 0), iota(square, 1)
    owner_row = jnp.sum(jnp.where(rows == cols, owner_col, 0.0), axis=0, keepdims=True)
    same = owner_col == owner_row
    earlier = jnp.where(same & (cols < rows), 1.0, 0.0)
    serve = serving.astype(jnp.float32)
    pair = jnp.where(
        jnp.floor((iota((group * n, n), 0) + 0.5) * (1.0 / group)) == iota((group * n, n), 1),
        1.0,
        0.0,
    )
    served = jnp.where(exact_dot(serve, pair, ((1,), (0,))) > 0.5, 1.0, 0.0)
    before = exact_dot(earlier, served, ((1,), (0,)))
    rank = jnp.sum(earlier, axis=1, keepdims=True)
    owner_u = jnp.sum(onehot * owner_col, axis=0, keepdims=True)
    rank_u = jnp.sum(onehot * rank, axis=0, keepdims=True)
    served_u = exact_dot(served, onehot, ((0,), (0,)))
    before_u = exact_dot(before, onehot, ((0,), (0,)))
    serve_u = exact_dot(serve, onehot, ((0,), (0,)))
    equal = exact_dot(onehot, onehot, ((0,), (0,)))
    both = (users, users)
    position = jnp.sum(
        jnp.where(iota(both, 0) < iota(both, 1), equal, 0.0), axis=0, keepdims=True
    )
    return owner_u, rank_u, served_u, before_u, serve_u, position


def first_kernel(
    n,
    chunks,
    ring_of,
    guess_hbm,
    received_ref,
    power_ref,
    noise_ref,
    gain_ref,
    cluster_ref,
    serving_ref,
    owner_ref,
    table_hbm,
    coef_all,
    solved_all,
    wrow_ref,
    rank_ref,
    guess,
    table,
    half,
    other,
    coef_send,
    coef_b,
    gains,
    pick,
    power_wide,
    smooth,
    cov,
    own,
    guess_sem,
    table_sem,
    half_send_sem,
    half_recv_sem,
    gain_send_sem,
    gain_recv_sem,
    coef_send_sem,
    coef_recv_sem,
    ring_send_sem,
    ring_recv_sem,
    local_sem,
):
    stations, antennas, _, users, tones = guess.shape
    pieces = stations * antennas
    block = PEER_MAX * CU
    clusters = serving_ref.shape[0]
    me = lax.axis_index("ap")
    part = lax.axis_index("sc")
    node, place = ring_of
    spot = place(me)
    right = node(lax.rem(spot + 1, n))
    left = node(lax.rem(spot + n - 1, n))

    table_copy = pltpu.make_async_copy(table_hbm.at[part], table, table_sem)
    table_copy.start()
    guess_copies = []
    for q in range(pieces):
        a, i = q // antennas, q % antennas
        copy = pltpu.make_async_copy(guess_hbm.at[a, i], guess.at[a, i], guess_sem.at[q])
        copy.start()
        guess_copies.append(copy)

    barrier = pltpu.get_barrier_semaphore()
    pl.semaphore_signal(barrier, inc=1, device_id={"sc": 1 - part}, device_id_type=MESH)
    for k in range(1, n):
        pl.semaphore_signal(
            barrier, inc=1, device_id={"ap": lax.rem(me + k, n)}, device_id_type=MESH
        )

    owner_u, rank_u, served_u, before_u, serve_u, position = user_tables(
        cluster_ref[...], serving_ref[...], owner_ref[...], clusters, users, stations, n
    )
    mef = me.astype(jnp.float32)
    mine = iota((n, users), 0) == mef
    served_me = jnp.sum(jnp.where(mine, served_u, 0.0), axis=0, keepdims=True)
    before_me = jnp.sum(jnp.where(mine, before_u, 0.0), axis=0, keepdims=True)
    target = jnp.where(
        served_me > 0.5, owner_u * block + before_me * CU + position, -1.0
    )
    pick[...] = jnp.where(iota((n * block, users), 0) == target, 1.0, 0.0).astype(jnp.bfloat16)
    wide = jnp.broadcast_to(power_ref[...] * (1.0 / users), (LANES, users))
    power_wide[...] = jnp.transpose(wide)

    pl.semaphore_wait(barrier, n)

    gain_copies = []
    for k in range(1, n):
        peer = lax.rem(me + k, n)
        copy = pltpu.make_async_remote_copy(
            src_ref=gain_ref,
            dst_ref=gains.at[me],
            send_sem=gain_send_sem.at[k],
            recv_sem=gain_recv_sem.at[n - k],
            device_id={"ap": peer},
            device_id_type=MESH,
        )
        copy.start()
        gain_copies.append(copy)
    gains[me] = gain_ref[...]

    table_copy.wait()
    half_copies = []
    contract = (((1,), (1,)), ((), ()))
    for q in range(pieces):
        a, i = q // antennas, q % antennas
        guess_copies[q].wait()
        sums = lax.dot_general(
            guess[a, i, 0], table[:, :tones], contract, preferred_element_type=jnp.float32
        ) + lax.dot_general(
            guess[a, i, 1], table[:, tones:], contract, preferred_element_type=jnp.float32
        )
        half[q] = (sums * (1.0 / TONE_NUMBER)).astype(jnp.bfloat16)
        copy = pltpu.make_async_remote_copy(
            src_ref=half.at[q],
            dst_ref=other.at[q],
            send_sem=half_send_sem.at[q],
            recv_sem=half_recv_sem.at[q],
            device_id={"sc": 1 - part},
            device_id_type=MESH,
        )
        copy.start()
        half_copies.append(copy)
    for q in range(pieces):
        half_copies[q].wait_recv()
        total = (half[q].astype(jnp.float32) + other[q].astype(jnp.float32)).astype(jnp.bfloat16)
        coef_b[pl.ds(q * users, users), :] = total
        chosen = jnp.dot(pick[...], total, preferred_element_type=jnp.float32)
        coef_send[:, q] = chosen.astype(jnp.bfloat16).reshape(n, block, 2 * TAPS)
    coef_copies = []
    for k in range(1, n):
        peer = lax.rem(me + k, n)
        copy = pltpu.make_async_remote_copy(
            src_ref=coef_send.at[peer],
            dst_ref=coef_all.at[me],
            send_sem=coef_send_sem.at[k],
            recv_sem=coef_recv_sem.at[n - k],
            device_id={"ap": peer},
            device_id_type=MESH,
        )
        copy.start()
        coef_copies.append(copy)
    own_coef = pltpu.make_async_copy(coef_send.at[me], coef_all.at[me], local_sem.at[chunks])
    own_coef.start()

    width = tones // chunks
    symbols = received_ref.shape[3]
    rows = stations * symbols
    ring_copies = {}
    reach = {}
    for c in range(chunks):
        far, near = n // 2, n - 1 - n // 2
        reach[c] = (far, near) if c % 2 == 0 else (near, far)

    def ring_start(c, direction, step):
        if step >= reach[c][direction]:
            return
        if step > 0:
            ring_copies[c, direction, step - 1].wait_recv()
        back = lax.rem(spot + n - step, n) if direction == 0 else lax.rem(spot + step, n)
        origin = node(back)
        source = own.at[c] if step == 0 else solved_all.at[origin, c]
        copy = pltpu.make_async_remote_copy(
            src_ref=source,
            dst_ref=solved_all.at[origin, c],
            send_sem=ring_send_sem.at[direction, c, step],
            recv_sem=ring_recv_sem.at[direction, c, step],
            device_id={"ap": right if direction == 0 else left},
            device_id_type=MESH,
        )
        copy.start()
        ring_copies[c, direction, step] = copy

    local_copies = []
    steps = max(max(r) for r in reach.values())
    entries = [(i, j) for i in range(antennas) for j in range(i + 1)]
    top = lax.broadcasted_iota(jnp.int32, (rows, 1), 0) < symbols
    noise = jnp.full((rows, 1), noise_ref[stations - 1], jnp.float32)
    for a in range(stations - 1):
        noise = jnp.where(
            (lax.broadcasted_iota(jnp.int32, (rows, 1), 0) // symbols) == a, noise_ref[a], noise
        )
    for c in range(chunks):
        base = c * width
        for reim in range(2):
            columns = table[:, reim * tones + base : reim * tones + base + width]
            smooth[reim] = jnp.dot(coef_b[...], columns, preferred_element_type=jnp.float32)
        for a in range(stations):
            for l in range(width // LANES):
                lanes = pl.ds(l * LANES, LANES)

                def body(step, sums, a=a, lanes=lanes):
                    sums = list(sums)
                    for w in range(2):
                        row = (step * 2 + w) * 8
                        scale = power_wide[pl.ds(pl.multiple_of(row, 8), 8), :]
                        re, im = [], []
                        for i in range(antennas):
                            at = pl.multiple_of((a * antennas + i) * users + row, 8)
                            re.append(smooth[0, pl.ds(at, 8), lanes])
                            im.append(smooth[1, pl.ds(at, 8), lanes])
                        at = 0
                        for i in range(antennas):
                            sre, sim = re[i] * scale, im[i] * scale
                            for j in range(i + 1):
                                sums[at] = sums[at] + (sre * re[j] + sim * im[j])
                                at += 1
                                if j < i:
                                    sums[at] = sums[at] + (sim * re[j] - sre * im[j])
                                    at += 1
                    return tuple(sums)

                zero = jnp.zeros((8, LANES), jnp.float32)
                sums = lax.fori_loop(0, users // 16, body, (zero,) * (antennas * antennas))
                for e in range(antennas * antennas):
                    value = jnp.sum(sums[e], axis=0, keepdims=True)
                    cov[e, a * symbols : (a + 1) * symbols, lanes] = jnp.broadcast_to(
                        value, (symbols, LANES)
                    )
        cov_re = [[None] * antennas for _ in range(antennas)]
        cov_im = [[None] * antennas for _ in range(antennas)]
        at = 0
        for i, j in entries:
            cov_re[i][j] = cov[at]
            at += 1
            if i == j:
                cov_re[i][j] = cov_re[i][j] + noise
            else:
                cov_im[i][j] = cov[at]
                at += 1
        signal = []
        for i in range(antennas):
            signal.append(
                tuple(
                    jnp.concatenate(
                        [
                            received_ref[a, i, reim, :, base : base + width].astype(jnp.float32)
                            for a in range(stations)
                        ],
                        axis=0,
                    )
                    for reim in range(2)
                )
            )
        solved = hermitian_solve(cov_re, cov_im, signal)
        for i in range(antennas):
            joined = jnp.concatenate([solved[i][0], solved[i][1]], axis=0)
            own[c, pl.ds(i * 2 * rows, 2 * rows), :] = joined.astype(jnp.bfloat16)
        copy = pltpu.make_async_copy(own.at[c], solved_all.at[me, c], local_sem.at[c])
        copy.start()
        local_copies.append(copy)
        for d in range(c + 1):
            for direction in range(2):
                ring_start(d, direction, c - d)
    for late in range(chunks, chunks + steps):
        for d in range(chunks):
            for direction in range(2):
                if late - d > 0:
                    ring_start(d, direction, late - d)

    for copy in gain_copies:
        copy.wait_recv()
    weights = []
    totals = jnp.zeros((1, users), jnp.float32)
    for p in range(n):
        for a in range(stations):
            row = serve_u[p * stations + a : p * stations + a + 1] * gains[p, a : a + 1, :]
            weights.append(row)
            totals = totals + row
    scale = 1.0 / (1.0 + totals)
    for p in range(n):
        goal = jnp.where(
            (owner_u == mef) & (served_u[p : p + 1] > 0.5),
            before_u[p : p + 1] * CU + position,
            -1.0,
        )
        hits = iota((block, users), 0) == goal
        for a in range(stations):
            value = jnp.sum(
                jnp.where(hits, weights[p * stations + a] * scale, 0.0), axis=1, keepdims=True
            )
            wrow_ref[p, a] = jnp.broadcast_to(value, (block, LANES))
        for k in range(PEER_MAX):
            value = jnp.sum(
                jnp.where(hits[k * CU : k * CU + 1], rank_u, 0.0), axis=1, keepdims=True
            )
            rank_ref[p * PEER_MAX + k : p * PEER_MAX + k + 1, :] = jnp.broadcast_to(
                value, (1, LANES)
            ).astype(jnp.int32)

    for copy in half_copies:
        copy.wait_send()
    for copy in gain_copies:
        copy.wait_send()
    for copy in coef_copies:
        copy.wait()
    own_coef.wait()
    for copy in local_copies:
        copy.wait()
    for (c, direction, step), copy in ring_copies.items():
        if step == reach[c][direction] - 1:
            copy.wait_recv()
        copy.wait_send()


def second_kernel(
    n, stations, antennas, rank_ref, coef_ref, wrow_ref, solved_ref, table_hbm, out_ref,
    table, solved, smooth, table_sem,
):
    width = solved_ref.shape[-1]
    tones = table.shape[-1] // 2
    block = PEER_MAX * CU
    symbols = out_ref.shape[1]
    rows = stations * symbols
    pieces = stations * antennas
    g = pl.program_id(0)

    @pl.when(g == 0)
    def _():
        copy = pltpu.make_async_copy(table_hbm.at[lax.axis_index("sc")], table, table_sem)
        copy.start()
        copy.wait()

    out_ref[...] = jnp.zeros_like(out_ref)

    def peer(p, carry):
        solved[...] = solved_ref[p, 0].astype(jnp.float32)
        coefs = coef_ref[p].reshape(pieces * block, 2 * TAPS)
        for reim in range(2):
            columns = table[:, pl.ds(pl.multiple_of(reim * tones + g * width, LANES), width)]
            smooth[reim] = jnp.dot(coefs, columns, preferred_element_type=jnp.float32)
        for l in range(width // LANES):
            lanes = pl.ds(l * LANES, LANES)
            sums = [[[None, None] for _ in range(symbols)] for _ in range(PEER_MAX)]
            for a in range(stations):
                weight = [wrow_ref[p, a, pl.ds(k * CU, CU), :] for k in range(PEER_MAX)]
                for i in range(antennas):
                    re, im = [], []
                    for k in range(PEER_MAX):
                        at = (a * antennas + i) * block + k * CU
                        re.append(smooth[0, pl.ds(at, CU), lanes] * weight[k])
                        im.append(smooth[1, pl.ds(at, CU), lanes] * weight[k])
                    for s in range(symbols):
                        first = i * 2 * rows + a * symbols + s
                        sre = solved[pl.ds(first, 1), lanes]
                        sim = solved[pl.ds(first + rows, 1), lanes]
                        for k in range(PEER_MAX):
                            new_re = re[k] * sre + im[k] * sim
                            new_im = re[k] * sim - im[k] * sre
                            old = sums[k][s]
                            if old[0] is not None:
                                new_re, new_im = old[0] + new_re, old[1] + new_im
                            sums[k][s] = [new_re, new_im]
            for k in range(PEER_MAX):
                slot = rank_ref[p * PEER_MAX + k, 0]
                for s in range(symbols):
                    for reim in range(2):
                        out_ref[slot, s, reim, :, lanes] += sums[k][s][reim]
        return carry

    lax.fori_loop(0, n, peer, 0)


def ring_functions(mesh):
    n = mesh.shape["ap"]
    half = n // 2

    def plain(q):
        return q

    def node(q):
        upper = q // half
        return (1 - upper) * 2 * q + upper * (2 * (n - q) - 1)

    def place(d):
        odd = d % 2
        return (1 - odd) * (d // 2) + odd * (n - (d + 1) // 2)

    if n % 2:
        return plain, plain
    try:
        axes = list(mesh.axis_names)
        line = np.moveaxis(mesh.devices, axes.index("ap"), 0).reshape(n, -1)[:, 0]
        spots = [tuple(d.coords) for d in line]
        sizes = [max(s[x] for s in spots) + 1 for x in range(3)]

        def length(order):
            far = 0
            for q in range(n):
                one, two = spots[order(q)], spots[order((q + 1) % n)]
                far += sum(
                    min(abs(one[x] - two[x]), sizes[x] - abs(one[x] - two[x])) for x in range(3)
                )
            return far

        if length(plain) < length(node):
            return plain, plain
    except (AttributeError, TypeError):
        pass
    return node, place


def local(
    n,
    parts,
    ring_of,
    unsmoothed_link_guesses,
    received,
    user_power,
    noise_power,
    ap_gain,
    user_cluster,
    serving,
    cluster_owner,
):
    stations, antennas, _, users, tones = unsmoothed_link_guesses.shape
    symbols = received.shape[3]
    pieces = stations * antennas
    block = PEER_MAX * CU
    rows = stations * symbols
    chunks = 4
    width = tones // chunks
    steps = n // 2
    table = jnp.asarray(delay_tables(parts, tones))
    vmem = pl.BlockSpec(memory_space=pltpu.VMEM)
    smem = pl.BlockSpec(memory_space=pltpu.SMEM)
    anywhere = pl.BlockSpec(memory_space=pl.ANY)
    dma = pltpu.SemaphoreType.DMA
    bf16, f32 = jnp.bfloat16, jnp.float32
    coef_all, solved_all, wrow, rank = pl.pallas_call(
        functools.partial(first_kernel, n, chunks, ring_of),
        out_shape=(
            jax.ShapeDtypeStruct((n, pieces, block, 2 * TAPS), bf16),
            jax.ShapeDtypeStruct((n, chunks, antennas * 2 * rows, width), bf16),
            jax.ShapeDtypeStruct((n, stations, block, LANES), f32),
            jax.ShapeDtypeStruct((n * PEER_MAX, LANES), jnp.int32),
        ),
        in_specs=[anywhere, vmem, vmem, smem, vmem, vmem, vmem, vmem, anywhere],
        out_specs=(anywhere, anywhere, vmem, vmem),
        scratch_shapes=[
            pltpu.VMEM((stations, antennas, 2, users, tones), bf16),
            pltpu.VMEM((2 * TAPS, 2 * tones), bf16),
            pltpu.VMEM((pieces, users, 2 * TAPS), bf16),
            pltpu.VMEM((pieces, users, 2 * TAPS), bf16),
            pltpu.VMEM((n, pieces, block, 2 * TAPS), bf16),
            pltpu.VMEM((pieces * users, 2 * TAPS), bf16),
            pltpu.VMEM((n, stations, users), f32),
            pltpu.VMEM((n * block, users), bf16),
            pltpu.VMEM((users, LANES), f32),
            pltpu.VMEM((2, pieces * users, width), f32),
            pltpu.VMEM((antennas * antennas, rows, width), f32),
            pltpu.VMEM((chunks, antennas * 2 * rows, width), bf16),
            dma((pieces,)),
            dma,
            dma((pieces,)),
            dma((pieces,)),
            dma((n,)),
            dma((n,)),
            dma((n,)),
            dma((n,)),
            dma((2, chunks, steps)),
            dma((2, chunks, steps)),
            dma((chunks + 1,)),
        ],
        compiler_params=pltpu.CompilerParams(
            collective_id=0, has_side_effects=True, vmem_limit_bytes=48 * 1024 * 1024
        ),
        name="smooth_and_solve",
    )(
        unsmoothed_link_guesses,
        received,
        user_power.reshape(1, users),
        noise_power,
        ap_gain,
        user_cluster.reshape(1, users),
        serving,
        cluster_owner,
        table,
    )
    combined = pl.pallas_call(
        functools.partial(second_kernel, n, stations, antennas),
        grid=(chunks,),
        out_shape=jax.ShapeDtypeStruct((OWN_MAX, symbols, 2, CU, tones), f32),
        in_specs=[
            smem,
            pl.BlockSpec((n, pieces, block, 2 * TAPS), lambda g: (0, 0, 0, 0)),
            pl.BlockSpec((n, stations, block, LANES), lambda g: (0, 0, 0, 0)),
            pl.BlockSpec((n, 1, antennas * 2 * rows, width), lambda g: (0, g, 0, 0)),
            anywhere,
        ],
        out_specs=pl.BlockSpec((OWN_MAX, symbols, 2, CU, width), lambda g: (0, 0, 0, 0, g)),
        scratch_shapes=[
            pltpu.VMEM((2 * TAPS, 2 * tones), bf16),
            pltpu.VMEM((antennas * 2 * rows, width), f32),
            pltpu.VMEM((2, pieces * block, width), f32),
            dma,
        ],
        name="combine",
    )(rank, coef_all, wrow, solved_all, table)
    return jnp.transpose(combined, (0, 3, 1, 2, 4))


def solution(mesh):
    placed = (
        P(("cell", "ap"), None, None, None, "sc"),
        P(("cell", "ap"), None, None, None, "sc"),
        P("cell"),
        P(("cell", "ap")),
        P(("cell", "ap"), None),
        P("cell"),
        P("cell", None),
        P("cell", None),
    )
    return jax.shard_map(
        functools.partial(local, mesh.shape["ap"], mesh.shape["sc"], ring_functions(mesh)),
        mesh=mesh,
        in_specs=placed,
        out_specs=P(("cell", "ap"), None, None, None, "sc"),
        check_vma=False,
    )
```

time: 180 us -> 65.9 us (0.37)
  waiting for transfers between devices: 82.9 us -> 0 us
  Pallas kernels: 0 us -> 53.4 us
  other arithmetic: 34.6 us -> 0 us
  blocking collectives: 22 us -> 0 us
  between operations: 13.8 us -> 0.04 us
  matrix products: 7.85 us -> 0 us
  local copies, waits for them, and re-layouts: 18.4 us -> 12.1 us
    reduce_scatter x1 -> x0, waiting for transfers between devices: 66.5 us -> none  [local(): lax.psum_scatter(picked * filled.astype(jnp.bfloat16)[:, None, None, None...]
    pallas_call x0 -> x2, Pallas kernels: none -> 53.4 us  [the longest x1 40.3 us: local(): pl.pallas_call(functools.partial(first_kernel, n, chunks, ring_of), out_s...]
    psum x1 -> x0, blocking collectives: 22 us -> none  [local(): totals = lax.psum(jnp.sum(weights, axis=0), 'ap')]
    psum x1 -> x0, waiting for transfers between devices: 16.4 us -> none  [local(): coefficients = lax.psum(combined.astype(jnp.bfloat16), 'sc')]
    gather x3 -> x0, local copies, waits for them, and re-layouts: 10.6 us -> none  [the longest x1 9.81 us: local(): picked = jnp.take(partial_value, member_rows.reshape(-1), axis=0)]
    add x4 -> x0, other arithmetic: 8.38 us -> none  [the longest x2 8.3 us: local_estimates(): est_re + smooth_re[i][:, None, :] * solved[i][0][None]]
    unnamed x18 -> x23, local copies, waits for them, and re-layouts: 0.83 us -> 9.1 us
    dot_general x5 -> x0, matrix products: 7.85 us -> none  [the longest x1 3.9 us: local(): jnp.dot(unsmoothed_link_guesses.reshape(-1, tone_positions), forward_tabl...]
  transfers between devices with their start and end apart: 2 -> 0, of which waited for: 2 -> 0; matrix products, arithmetic and copies ran while one was open for 3% -> 0% of each run, Pallas kernels for 0% -> 0%
where the time goes in v1:
time: 65.9 us; the launch traced here: 65.6 us
  Pallas kernels  53.4 us (81%)
  local copies, waits for them, and re-layouts  12.1 us (18%)
    pallas_call x1, Pallas kernels, local(): pl.pallas_call(functools.partial(first_kernel, n, chunks, ring_of), out_s...  40.3 us
    pallas_call x1, Pallas kernels, local(): pl.pallas_call(functools.partial(second_kernel, n, stations, antennas), g...  13.1 us
    unnamed x23, local copies, waits for them, and re-layouts  9.1 us
    transpose x1, local copies, waits for them, and re-layouts, local(): return jnp.transpose(combined, (0, 3, 1, 2, 4))  3 us

profile of v1, /device:TPU:0, one launch (start us, length us, event | category | flops | bytes accessed | tf_op | source)
XLA Modules:
  0.0 65.6 jit_solution(15062480290202417845)
XLA Ops:
  0.0 0.7 %copy.10.owner_ref = s32[16,1]{1,0:T(8,128)S(1)} copy(s32[16,1]{0,1:T(1,128)} %param.16) | data formatting | bytes 128 | tf_op args[7]
  0.7 0.0 copy-start
  0.7 1.2 %copy-done = bf16[2,128,2048]{2,1,0:T(8,128)(2,1)S(1)} copy-done((bf16[2,128,2048]{2,1,0:T(8,128)(2,1)S(1)}, bf16[2,128,2048]{2,1,0:T(8,128)(2,1)}, u32[]{:S(2)}) %copy-start) | copy-done | bytes 1048600
  2.0 0.0 copy-start.4
  2.0 0.9 %copy-done.4 = bf16[2,4,2,4,1024]{4,3,2,1,0:T(4,128)(2,1)S(1)} copy-done((bf16[2,4,2,4,1024]{4,3,2,1,0:T(4,128)(2,1)S(1)}, bf16[2,4,2,4,1024]{4,3,2,1,0:T(4,128)(2,1)}, u32[]{:S(2)}) %copy-start.4) | copy-done | bytes 131096
  2.9 0.0 copy-start.6
  2.9 0.7 %copy-done.6 = s32[16,16]{1,0:T(8,128)S(1)} copy-done((s32[16,16]{1,0:T(8,128)S(1)}, s32[16,16]{1,0:T(8,128)}, u32[]{:S(2)}) %copy-start.6) | copy-done | bytes 1048
  3.6 0.0 copy-start.7
  3.6 0.7 %copy-done.7 = f32[2,128]{1,0:T(2,128)S(1)} copy-done((f32[2,128]{1,0:T(2,128)S(1)}, f32[2,128]{1,0:T(2,128)}, u32[]{:S(2)}) %copy-start.7) | copy-done | bytes 1048
  4.2 0.0 copy-start.8
  4.2 0.7 copy-done.8
  4.9 0.0 copy-start.9
  4.9 0.7 copy-done.9
  5.6 0.0 copy-start.10
  5.6 0.7 copy-done.10
  6.2 40.3 %smooth_and_solve.1 = (bf16[8,8,16,128]{3,2,1,0:T(8,128)(2,1)S(1)}, bf16[8,4,64,256]{3,2,1,0:T(8,128)(2,1)S(1)}, f32[8,2,16,128]{3,2,1,0:T(8,128)S(1)}, s32[16,128]{1,0:T(8,128)S(1)}) custom-call(bf16[2,4,2,128,1024]{4,3,2,1,0:T(8,128)(2,1)} %guess_hbm.1, bf16[2,4,2,4,1024]{4,3,2,1,0:T(4,128)(2,1)S(1)} %copy-done.4, f32[1,128]{1,0:T(1,128)S(1)} %bitcast.3, ...), custom_call_target="tpu_custom_call" | custom-call | tf_op jit(solution)/shard_map/smooth_and_solve/pallas_call | solution.py:558
  46.5 0.0 copy-start.1
  46.5 1.0 %copy-done.1 = bf16[8,4,64,256]{3,2,1,0:T(8,128)(2,1)} copy-done((bf16[8,4,64,256]{3,2,1,0:T(8,128)(2,1)}, bf16[8,4,64,256]{3,2,1,0:T(8,128)(2,1)S(1)}, u32[]{:S(2)}) %copy-start.1) | copy-done | bytes 1048600
  47.5 0.0 copy-start.2
  47.5 0.7 %copy-done.2 = bf16[8,8,16,128]{3,2,1,0:T(8,128)(2,1)} copy-done((bf16[8,8,16,128]{3,2,1,0:T(8,128)(2,1)}, bf16[8,8,16,128]{3,2,1,0:T(8,128)(2,1)S(1)}, u32[]{:S(2)}) %copy-start.2) | copy-done | bytes 262168
  48.2 0.0 copy-start.3
  48.2 0.6 copy-done.3
  48.8 0.0 copy-start.5
  48.8 0.6 copy-done.5
  49.4 13.1 %combine.1 = f32[4,4,2,8,1024]{4,3,2,1,0:T(8,128)} custom-call(s32[16,128]{1,0:T(8,128)} %copy-done.5, bf16[8,8,16,128]{3,2,1,0:T(8,128)(2,1)} %copy-done.2, f32[8,2,16,128]{3,2,1,0:T(8,128)} %copy-done.3, bf16[8,4,64,256]{3,2,1,0:T(8,128)(2,1)} %copy-done.1, bf16[2,128,2048]{2,1,0:T(8,128)(2,1)} %constant.2.clone.table_hbm), custom_call_target="tpu_custom_call" | custom-call | tf_op jit(solution)/shard_map/combine/pallas_call | solution.py:608
  62.6 3.0 %copy.11 = f32[4,8,4,2,1024]{4,3,2,1,0:T(2,128)} copy(f32[4,8,4,2,1024]{4,1,3,2,0:T(8,128)} %bitcast.5) | data formatting | bytes 2097152 | tf_op jit(solution)/shard_map/transpose | solution.py:628
Async XLA Ops:
  0.7 1.2 %copy-start = (bf16[2,128,2048]{2,1,0:T(8,128)(2,1)S(1)}, bf16[2,128,2048]{2,1,0:T(8,128)(2,1)}, u32[]{:S(2)}) copy-start(bf16[2,128,2048]{2,1,0:T(8,128)(2,1)} %constant.2.clone.table_hbm) | copy-start | bytes 3145732
  2.0 0.9 %copy-start.4 = (bf16[2,4,2,4,1024]{4,3,2,1,0:T(4,128)(2,1)S(1)}, bf16[2,4,2,4,1024]{4,3,2,1,0:T(4,128)(2,1)}, u32[]{:S(2)}) copy-start(bf16[2,4,2,4,1024]{4,3,2,1,0:T(4,128)(2,1)} %received_ref.1) | copy-start | bytes 393220
  2.9 0.7 %copy-start.6 = (s32[16,16]{1,0:T(8,128)S(1)}, s32[16,16]{1,0:T(8,128)}, u32[]{:S(2)}) copy-start(s32[16,16]{1,0:T(8,128)} %serving_ref.1) | copy-start | bytes 3076
  3.6 0.7 %copy-start.7 = (f32[2,128]{1,0:T(2,128)S(1)}, f32[2,128]{1,0:T(2,128)}, u32[]{:S(2)}) copy-start(f32[2,128]{1,0:T(2,128)} %gain_ref.1) | copy-start | bytes 3076
  4.2 0.7 copy-start.8
  4.9 0.7 copy-start.9
  5.6 0.7 copy-start.10
  46.5 1.0 %copy-start.1 = (bf16[8,4,64,256]{3,2,1,0:T(8,128)(2,1)}, bf16[8,4,64,256]{3,2,1,0:T(8,128)(2,1)S(1)}, u32[]{:S(2)}) copy-start(bf16[8,4,64,256]{3,2,1,0:T(8,128)(2,1)S(1)} %get-tuple-element.12.solved_ref) | copy-start | bytes 3145732
  47.5 0.7 %copy-start.2 = (bf16[8,8,16,128]{3,2,1,0:T(8,128)(2,1)}, bf16[8,8,16,128]{3,2,1,0:T(8,128)(2,1)S(1)}, u32[]{:S(2)}) copy-start(bf16[8,8,16,128]{3,2,1,0:T(8,128)(2,1)S(1)} %get-tuple-element.10.coef_ref) | copy-start | bytes 786436
  48.2 0.6 copy-start.3
  48.8 0.6 copy-start.5

commit v2 on v1

--- a/solution.py
+++ b/solution.py
@@ -100,10 +100,10 @@
 
 def user_tables(user_cluster, serving, owner, clusters, users, group, n):
     onehot = (iota((clusters, users), 0) == user_cluster.astype(jnp.float32)).astype(jnp.float32)
-    owner_col = owner.astype(jnp.float32)
+    owner_row = owner.astype(jnp.float32)
     square = (clusters, clusters)
     rows, cols = iota(square, 0), iota(square, 1)
-    owner_row = jnp.sum(jnp.where(rows == cols, owner_col, 0.0), axis=0, keepdims=True)
+    owner_col = jnp.sum(jnp.where(rows == cols, owner_row, 0.0), axis=1, keepdims=True)
     same = owner_col == owner_row
     earlier = jnp.where(same & (cols < rows), 1.0, 0.0)
     serve = serving.astype(jnp.float32)
@@ -133,6 +133,19 @@
     chunks,
     ring_of,
     guess_hbm,
+    received_hbm,
+    power_hbm,
+    noise_hbm,
+    gain_hbm,
+    cluster_hbm,
+    serving_hbm,
+    owner_hbm,
+    table_hbm,
+    share_ref,
+    rank_ref,
+    coef_all,
+    solved_all,
+    wrow_ref,
     received_ref,
     power_ref,
     noise_ref,
@@ -140,11 +153,7 @@
     cluster_ref,
     serving_ref,
     owner_ref,
-    table_hbm,
-    coef_all,
-    solved_all,
-    wrow_ref,
-    rank_ref,
+    solved_wide,
     guess,
     table,
     half,
@@ -168,6 +177,7 @@
     ring_send_sem,
     ring_recv_sem,
     local_sem,
+    small_sem,
 ):
     stations, antennas, _, users, tones = guess.shape
     pieces = stations * antennas
@@ -182,6 +192,19 @@
 
     table_copy = pltpu.make_async_copy(table_hbm.at[part], table, table_sem)
     table_copy.start()
+    small_copies = []
+    for source, into in (
+        (cluster_hbm, cluster_ref),
+        (serving_hbm, serving_ref),
+        (owner_hbm, owner_ref),
+        (power_hbm, power_ref),
+        (gain_hbm, gain_ref),
+        (noise_hbm, noise_ref),
+        (received_hbm, received_ref),
+    ):
+        copy = pltpu.make_async_copy(source, into, small_sem.at[len(small_copies)])
+        copy.start()
+        small_copies.append(copy)
     guess_copies = []
     for q in range(pieces):
         a, i = q // antennas, q % antennas
@@ -196,6 +219,8 @@
             barrier, inc=1, device_id={"ap": lax.rem(me + k, n)}, device_id_type=MESH
         )
 
+    for copy in small_copies:
+        copy.wait()
     owner_u, rank_u, served_u, before_u, serve_u, position = user_tables(
         cluster_ref[...], serving_ref[...], owner_ref[...], clusters, users, stations, n
     )
@@ -268,7 +293,7 @@
         )
         copy.start()
         coef_copies.append(copy)
-    own_coef = pltpu.make_async_copy(coef_send.at[me], coef_all.at[me], local_sem.at[chunks])
+    own_coef = pltpu.make_async_copy(coef_send.at[me], coef_all.at[me], local_sem)
     own_coef.start()
 
     width = tones // chunks
@@ -280,14 +305,23 @@
         far, near = n // 2, n - 1 - n // 2
         reach[c] = (far, near) if c % 2 == 0 else (near, far)
 
+    ready = []
+
+    def origin_of(direction, step):
+        back = lax.rem(spot + n - step, n) if direction == 0 else lax.rem(spot + step, n)
+        return node(back)
+
     def ring_start(c, direction, step):
-        if step >= reach[c][direction]:
+        if step > reach[c][direction]:
             return
+        origin = origin_of(direction, step)
+        source = own.at[c]
         if step > 0:
             ring_copies[c, direction, step - 1].wait_recv()
-        back = lax.rem(spot + n - step, n) if direction == 0 else lax.rem(spot + step, n)
-        origin = node(back)
-        source = own.at[c] if step == 0 else solved_all.at[origin, c]
+            source = solved_all.at[origin, c]
+            ready.append((origin, c, source))
+        if step == reach[c][direction]:
+            return
         copy = pltpu.make_async_remote_copy(
             src_ref=source,
             dst_ref=solved_all.at[origin, c],
@@ -299,15 +333,15 @@
         copy.start()
         ring_copies[c, direction, step] = copy
 
-    local_copies = []
     steps = max(max(r) for r in reach.values())
     entries = [(i, j) for i in range(antennas) for j in range(i + 1)]
-    top = lax.broadcasted_iota(jnp.int32, (rows, 1), 0) < symbols
-    noise = jnp.full((rows, 1), noise_ref[stations - 1], jnp.float32)
-    for a in range(stations - 1):
-        noise = jnp.where(
-            (lax.broadcasted_iota(jnp.int32, (rows, 1), 0) // symbols) == a, noise_ref[a], noise
-        )
+    noise = jnp.concatenate(
+        [
+            jnp.broadcast_to(noise_ref[0:1, a : a + 1], (symbols, 1))
+            for a in range(stations)
+        ],
+        axis=0,
+    )
     for c in range(chunks):
         base = c * width
         for reim in range(2):
@@ -374,17 +408,10 @@
         for i in range(antennas):
             joined = jnp.concatenate([solved[i][0], solved[i][1]], axis=0)
             own[c, pl.ds(i * 2 * rows, 2 * rows), :] = joined.astype(jnp.bfloat16)
-        copy = pltpu.make_async_copy(own.at[c], solved_all.at[me, c], local_sem.at[c])
-        copy.start()
-        local_copies.append(copy)
+        ready.append((me, c, own.at[c]))
         for d in range(c + 1):
             for direction in range(2):
                 ring_start(d, direction, c - d)
-    for late in range(chunks, chunks + steps):
-        for d in range(chunks):
-            for direction in range(2):
-                if late - d > 0:
-                    ring_start(d, direction, late - d)
 
     for copy in gain_copies:
         copy.wait_recv()
@@ -416,52 +443,26 @@
                 value, (1, LANES)
             ).astype(jnp.int32)
 
-    for copy in half_copies:
-        copy.wait_send()
-    for copy in gain_copies:
-        copy.wait_send()
+
     for copy in coef_copies:
-        copy.wait()
+        copy.wait_recv()
     own_coef.wait()
-    for copy in local_copies:
-        copy.wait()
-    for (c, direction, step), copy in ring_copies.items():
-        if step == reach[c][direction] - 1:
-            copy.wait_recv()
-        copy.wait_send()
-
-
-def second_kernel(
-    n, stations, antennas, rank_ref, coef_ref, wrow_ref, solved_ref, table_hbm, out_ref,
-    table, solved, smooth, table_sem,
-):
-    width = solved_ref.shape[-1]
-    tones = table.shape[-1] // 2
-    block = PEER_MAX * CU
-    symbols = out_ref.shape[1]
-    rows = stations * symbols
-    pieces = stations * antennas
-    g = pl.program_id(0)
-
-    @pl.when(g == 0)
-    def _():
-        copy = pltpu.make_async_copy(table_hbm.at[lax.axis_index("sc")], table, table_sem)
-        copy.start()
-        copy.wait()
-
-    out_ref[...] = jnp.zeros_like(out_ref)
-
-    def peer(p, carry):
-        solved[...] = solved_ref[p, 0].astype(jnp.float32)
-        coefs = coef_ref[p].reshape(pieces * block, 2 * TAPS)
+
+    def combine(origin, c, source):
+        base = c * width
+        solved_wide[...] = source[...].astype(jnp.float32)
+        coefs = coef_all[origin].reshape(pieces * block, 2 * TAPS)
         for reim in range(2):
-            columns = table[:, pl.ds(pl.multiple_of(reim * tones + g * width, LANES), width)]
-            smooth[reim] = jnp.dot(coefs, columns, preferred_element_type=jnp.float32)
-        for l in range(width // LANES):
-            lanes = pl.ds(l * LANES, LANES)
+            columns = table[:, reim * tones + base : reim * tones + base + width]
+            smooth[reim, : pieces * block, :] = jnp.dot(
+                coefs, columns, preferred_element_type=jnp.float32
+            )
+
+        def tile(l, carry):
+            lanes = pl.ds(pl.multiple_of(l * LANES, LANES), LANES)
             sums = [[[None, None] for _ in range(symbols)] for _ in range(PEER_MAX)]
             for a in range(stations):
-                weight = [wrow_ref[p, a, pl.ds(k * CU, CU), :] for k in range(PEER_MAX)]
+                weight = [wrow_ref[origin, a, pl.ds(k * CU, CU), :] for k in range(PEER_MAX)]
                 for i in range(antennas):
                     re, im = [], []
                     for k in range(PEER_MAX):
@@ -470,8 +471,8 @@
                         im.append(smooth[1, pl.ds(at, CU), lanes] * weight[k])
                     for s in range(symbols):
                         first = i * 2 * rows + a * symbols + s
-                        sre = solved[pl.ds(first, 1), lanes]
-                        sim = solved[pl.ds(first + rows, 1), lanes]
+                        sre = solved_wide[pl.ds(first, 1), lanes]
+                        sim = solved_wide[pl.ds(first + rows, 1), lanes]
                         for k in range(PEER_MAX):
                             new_re = re[k] * sre + im[k] * sim
                             new_im = re[k] * sim - im[k] * sre
@@ -480,13 +481,73 @@
                                 new_re, new_im = old[0] + new_re, old[1] + new_im
                             sums[k][s] = [new_re, new_im]
             for k in range(PEER_MAX):
-                slot = rank_ref[p * PEER_MAX + k, 0]
                 for s in range(symbols):
                     for reim in range(2):
-                        out_ref[slot, s, reim, :, lanes] += sums[k][s][reim]
+                        share_ref[
+                            c * (width // LANES) + l,
+                            origin * PEER_MAX + k,
+                            pl.ds((s * 2 + reim) * CU, CU),
+                            :,
+                        ] = sums[k][s][reim]
+            return carry
+
+        lax.fori_loop(0, width // LANES, tile, 0)
+
+    def drain(most):
+        for _ in range(most):
+            if ready:
+                combine(*ready.pop(0))
+
+    drain(2)
+    for late in range(chunks, chunks + steps + 1):
+        for d in range(chunks):
+            for direction in range(2):
+                if late - d > 0:
+                    ring_start(d, direction, late - d)
+            drain(2)
+    drain(len(ready))
+
+    for copy in half_copies:
+        copy.wait_send()
+    for copy in gain_copies:
+        copy.wait_send()
+    for copy in coef_copies:
+        copy.wait_send()
+    for copy in ring_copies.values():
+        copy.wait_send()
+
+
+def second_kernel(n, rank_ref, share_ref, out_hbm, total, moved, out_sem):
+    tiles, _, rows, _ = share_ref.shape
+    pairs = rows // (2 * CU)
+    height = CU * pairs * tiles * 2
+    total[...] = jnp.zeros_like(total)
+    slots = [rank_ref[k, 0] for k in range(n * PEER_MAX)]
+
+    def tile(l, carry):
+        for k in range(n * PEER_MAX):
+            total[l, slots[k]] += share_ref[l, k]
         return carry
 
-    lax.fori_loop(0, n, peer, 0)
+    lax.fori_loop(0, tiles, tile, 0)
+    copies = []
+    for r in range(OWN_MAX):
+
+        def move(l, carry, r=r):
+            for s in range(pairs):
+                for reim in range(2):
+                    moved[pl.ds(r * height + (s * tiles + l) * 2 + reim, CU, stride=pairs * tiles * 2), :] = (
+                        total[l, r, pl.ds((s * 2 + reim) * CU, CU), :]
+                    )
+            return carry
+
+        lax.fori_loop(0, tiles, move, 0)
+        part = pl.ds(r * height, height)
+        copy = pltpu.make_async_copy(moved.at[part], out_hbm.at[part], out_sem.at[r])
+        copy.start()
+        copies.append(copy)
+    for copy in copies:
+        copy.wait()
 
 
 def ring_functions(mesh):
@@ -555,17 +616,28 @@
     anywhere = pl.BlockSpec(memory_space=pl.ANY)
     dma = pltpu.SemaphoreType.DMA
     bf16, f32 = jnp.bfloat16, jnp.float32
-    coef_all, solved_all, wrow, rank = pl.pallas_call(
+    hbm = pl.BlockSpec(memory_space=pltpu.HBM)
+    tiles = tones // LANES
+    share, rank = pl.pallas_call(
         functools.partial(first_kernel, n, chunks, ring_of),
         out_shape=(
-            jax.ShapeDtypeStruct((n, pieces, block, 2 * TAPS), bf16),
-            jax.ShapeDtypeStruct((n, chunks, antennas * 2 * rows, width), bf16),
-            jax.ShapeDtypeStruct((n, stations, block, LANES), f32),
+            jax.ShapeDtypeStruct((tiles, n * PEER_MAX, symbols * 2 * CU, LANES), f32),
             jax.ShapeDtypeStruct((n * PEER_MAX, LANES), jnp.int32),
         ),
-        in_specs=[anywhere, vmem, vmem, smem, vmem, vmem, vmem, vmem, anywhere],
-        out_specs=(anywhere, anywhere, vmem, vmem),
+        in_specs=[hbm] * 9,
+        out_specs=(vmem, vmem),
         scratch_shapes=[
+            pltpu.VMEM((n, pieces, block, 2 * TAPS), bf16),
+            pltpu.VMEM((n, chunks, antennas * 2 * rows, width), bf16),
+            pltpu.VMEM((n, stations, block, LANES), f32),
+            pltpu.VMEM(received.shape, bf16),
+            pltpu.VMEM((1, users), f32),
+            pltpu.VMEM((1, stations), f32),
+            pltpu.VMEM((stations, users), f32),
+            pltpu.VMEM((1, users), jnp.int32),
+            pltpu.VMEM(serving.shape, jnp.int32),
+            pltpu.VMEM((1, serving.shape[0]), jnp.int32),
+            pltpu.VMEM((antennas * 2 * rows, width), f32),
             pltpu.VMEM((stations, antennas, 2, users, tones), bf16),
             pltpu.VMEM((2 * TAPS, 2 * tones), bf16),
             pltpu.VMEM((pieces, users, 2 * TAPS), bf16),
@@ -588,44 +660,41 @@
             dma((n,)),
             dma((2, chunks, steps)),
             dma((2, chunks, steps)),
-            dma((chunks + 1,)),
+            dma,
+            dma((7,)),
         ],
         compiler_params=pltpu.CompilerParams(
-            collective_id=0, has_side_effects=True, vmem_limit_bytes=48 * 1024 * 1024
+            collective_id=0, has_side_effects=True, vmem_limit_bytes=40 * 1024 * 1024
         ),
-        name="smooth_and_solve",
+        name="smooth_solve_combine",
     )(
         unsmoothed_link_guesses,
         received,
         user_power.reshape(1, users),
-        noise_power,
+        noise_power.reshape(1, stations),
         ap_gain,
         user_cluster.reshape(1, users),
         serving,
-        cluster_owner,
+        cluster_owner.reshape(1, -1),
         table,
     )
-    combined = pl.pallas_call(
-        functools.partial(second_kernel, n, stations, antennas),
-        grid=(chunks,),
-        out_shape=jax.ShapeDtypeStruct((OWN_MAX, symbols, 2, CU, tones), f32),
-        in_specs=[
-            smem,
-            pl.BlockSpec((n, pieces, block, 2 * TAPS), lambda g: (0, 0, 0, 0)),
-            pl.BlockSpec((n, stations, block, LANES), lambda g: (0, 0, 0, 0)),
-            pl.BlockSpec((n, 1, antennas * 2 * rows, width), lambda g: (0, g, 0, 0)),
-            anywhere,
+    lines = OWN_MAX * CU * symbols * tiles * 2
+    placed = pl.pallas_call(
+        functools.partial(second_kernel, n),
+        out_shape=jax.ShapeDtypeStruct((lines, LANES), f32),
+        in_specs=[smem, vmem],
+        out_specs=hbm,
+        scratch_shapes=[
+            pltpu.VMEM((tiles, OWN_MAX, symbols * 2 * CU, LANES), f32),
+            pltpu.VMEM((lines, LANES), f32),
+            dma((OWN_MAX,)),
         ],
-        out_specs=pl.BlockSpec((OWN_MAX, symbols, 2, CU, width), lambda g: (0, 0, 0, 0, g)),
-        scratch_shapes=[
-            pltpu.VMEM((2 * TAPS, 2 * tones), bf16),
-            pltpu.VMEM((antennas * 2 * rows, width), f32),
-            pltpu.VMEM((2, pieces * block, width), f32),
-            dma,
-        ],
-        name="combine",
-    )(rank, coef_all, wrow, solved_all, table)
-    return jnp.transpose(combined, (0, 3, 1, 2, 4))
+        compiler_params=pltpu.CompilerParams(vmem_limit_bytes=16 * 1024 * 1024),
+        name="place",
+    )(rank, share)
+    placed = placed.reshape(OWN_MAX, CU, symbols, tiles, 2, LANES)
+    placed = jnp.transpose(placed, (0, 1, 2, 4, 3, 5))
+    return placed.reshape(OWN_MAX, CU, symbols, 2, tones)
 
 
 def solution(mesh):

time: 65.9 us -> 52.6 us (0.80)
  Pallas kernels: 53.4 us -> 44.1 us
  local copies, waits for them, and re-layouts: 12.1 us -> 8.31 us
    pallas_call x1, Pallas kernels: 13.1 us -> 3.13 us  [local(): pl.pallas_call(functools.partial(second_kernel, n), out_shape=jax.ShapeDt...]
    transpose x1 -> x0, local copies, waits for them, and re-layouts: 3 us -> none  [local(): return jnp.transpose(combined, (0, 3, 1, 2, 4))]
    unnamed x23 -> x18, local copies, waits for them, and re-layouts: 9.1 us -> 8.31 us
where the time goes in v2:
time: 52.6 us; the launch traced here: 52.4 us
  Pallas kernels  44.1 us (84%)
  local copies, waits for them, and re-layouts  8.31 us (16%)
    pallas_call x1, Pallas kernels, local(): pl.pallas_call(functools.partial(first_kernel, n, chunks, ring_of), out_s...  40.9 us
    unnamed x18, local copies, waits for them, and re-layouts  8.31 us
    pallas_call x1, Pallas kernels, local(): pl.pallas_call(functools.partial(second_kernel, n), out_shape=jax.ShapeDt...  3.13 us

profile of v2, /device:TPU:0, one launch (start us, length us, event | category | flops | bytes accessed | tf_op | source)
XLA Modules:
  0.0 52.4 jit_solution(2517928005076106702)
XLA Ops:
  0.0 0.0 copy-start
  0.0 2.2 %copy-done = bf16[2,4,2,128,1024]{4,3,2,1,0:T(8,128)(2,1)S(1)} copy-done((bf16[2,4,2,128,1024]{4,3,2,1,0:T(8,128)(2,1)S(1)}, bf16[2,4,2,128,1024]{4,3,2,1,0:T(8,128)(2,1)}, u32[]{:S(2)}) %copy-start) | copy-done | bytes 4194328
  2.2 0.0 copy-start.1
  2.2 1.2 %copy-done.1 = bf16[2,128,2048]{2,1,0:T(8,128)(2,1)S(1)} copy-done((bf16[2,128,2048]{2,1,0:T(8,128)(2,1)S(1)}, bf16[2,128,2048]{2,1,0:T(8,128)(2,1)}, u32[]{:S(2)}) %copy-start.1) | copy-done | bytes 1048600
  3.4 0.0 copy-start.2
  3.4 0.9 %copy-done.2 = bf16[2,4,2,4,1024]{4,3,2,1,0:T(4,128)(2,1)S(1)} copy-done((bf16[2,4,2,4,1024]{4,3,2,1,0:T(4,128)(2,1)S(1)}, bf16[2,4,2,4,1024]{4,3,2,1,0:T(4,128)(2,1)}, u32[]{:S(2)}) %copy-start.2) | copy-done | bytes 131096
  4.3 0.0 copy-start.3
  4.3 0.7 %copy-done.3 = s32[16,16]{1,0:T(8,128)S(1)} copy-done((s32[16,16]{1,0:T(8,128)S(1)}, s32[16,16]{1,0:T(8,128)}, u32[]{:S(2)}) %copy-start.3) | copy-done | bytes 1048
  5.0 0.0 copy-start.4
  5.0 0.7 %copy-done.4 = f32[2,128]{1,0:T(2,128)S(1)} copy-done((f32[2,128]{1,0:T(2,128)S(1)}, f32[2,128]{1,0:T(2,128)}, u32[]{:S(2)}) %copy-start.4) | copy-done | bytes 1048
  5.7 0.0 copy-start.5
  5.7 0.7 %copy-done.5 = f32[128]{0:T(128)S(1)} copy-done((f32[128]{0:T(128)S(1)}, f32[128]{0:T(128)}, u32[]{:S(2)}) %copy-start.5) | copy-done | bytes 536
  6.4 0.0 copy-start.6
  6.4 0.7 %copy-done.6 = f32[2]{0:T(128)S(1)} copy-done((f32[2]{0:T(128)S(1)}, f32[2]{0:T(128)}, u32[]{:S(2)}) %copy-start.6) | copy-done | bytes 32
  7.0 0.0 copy-start.7
  7.0 0.7 %copy-done.7 = s32[128]{0:T(128)S(1)} copy-done((s32[128]{0:T(128)S(1)}, s32[128]{0:T(128)}, u32[]{:S(2)}) %copy-start.7) | copy-done | bytes 536
  7.7 0.0 copy-start.8
  7.7 0.7 %copy-done.8 = s32[16,1]{0,1:T(1,128)S(1)} copy-done((s32[16,1]{0,1:T(1,128)S(1)}, s32[16,1]{0,1:T(1,128)}, u32[]{:S(2)}) %copy-start.8) | copy-done | bytes 88
  8.3 40.9 %smooth_solve_combine.1 = (f32[8,16,64,128]{3,2,1,0:T(8,128)S(1)}, s32[16,128]{1,0:T(8,128)S(1)}) custom-call(bf16[2,4,2,128,1024]{4,3,2,1,0:T(8,128)(2,1)S(1)} %copy-done, bf16[2,4,2,4,1024]{4,3,2,1,0:T(4,128)(2,1)S(1)} %copy-done.2, f32[1,128]{1,0:T(1,128)S(1)} %bitcast.9, f32[1,2]{1,0:T(1,128)S(1)} %bitcast.10, f32[2,128]{1,0:T(2,128)S(1)} %copy-done.4, ...), custom_call_target="tpu_custom_call" | custom-call | tf_op jit(solution)/shard_map/smooth_solve_combine/pallas_call | solution.py:621
  49.3 3.1 %place.1 = f32[2048,128]{1,0:T(8,128)} custom-call(s32[16,128]{1,0:T(8,128)S(1)} %get-tuple-element.7.rank_ref, f32[8,16,64,128]{3,2,1,0:T(8,128)S(1)} %get-tuple-element.8.share_ref), custom_call_target="tpu_custom_call" | custom-call | tf_op jit(solution)/shard_map/place/pallas_call | solution.py:682
Async XLA Ops:
  0.0 2.2 %copy-start = (bf16[2,4,2,128,1024]{4,3,2,1,0:T(8,128)(2,1)S(1)}, bf16[2,4,2,128,1024]{4,3,2,1,0:T(8,128)(2,1)}, u32[]{:S(2)}) copy-start(bf16[2,4,2,128,1024]{4,3,2,1,0:T(8,128)(2,1)} %guess_hbm.1) | copy-start | bytes 12582916
  2.2 1.2 %copy-start.1 = (bf16[2,128,2048]{2,1,0:T(8,128)(2,1)S(1)}, bf16[2,128,2048]{2,1,0:T(8,128)(2,1)}, u32[]{:S(2)}) copy-start(bf16[2,128,2048]{2,1,0:T(8,128)(2,1)} %constant.2.clone.table_hbm) | copy-start | bytes 3145732
  3.4 0.9 %copy-start.2 = (bf16[2,4,2,4,1024]{4,3,2,1,0:T(4,128)(2,1)S(1)}, bf16[2,4,2,4,1024]{4,3,2,1,0:T(4,128)(2,1)}, u32[]{:S(2)}) copy-start(bf16[2,4,2,4,1024]{4,3,2,1,0:T(4,128)(2,1)} %received_hbm.1) | copy-start | bytes 393220
  4.3 0.7 %copy-start.3 = (s32[16,16]{1,0:T(8,128)S(1)}, s32[16,16]{1,0:T(8,128)}, u32[]{:S(2)}) copy-start(s32[16,16]{1,0:T(8,128)} %serving_hbm.1) | copy-start | bytes 3076
  5.0 0.7 %copy-start.4 = (f32[2,128]{1,0:T(2,128)S(1)}, f32[2,128]{1,0:T(2,128)}, u32[]{:S(2)}) copy-start(f32[2,128]{1,0:T(2,128)} %gain_hbm.1) | copy-start | bytes 3076
  5.7 0.7 %copy-start.5 = (f32[128]{0:T(128)S(1)}, f32[128]{0:T(128)}, u32[]{:S(2)}) copy-start(f32[128]{0:T(128)} %param.11) | copy-start | bytes 1540
  6.4 0.7 %copy-start.6 = (f32[2]{0:T(128)S(1)}, f32[2]{0:T(128)}, u32[]{:S(2)}) copy-start(f32[2]{0:T(128)} %param.12) | copy-start | bytes 28
  7.0 0.7 %copy-start.7 = (s32[128]{0:T(128)S(1)}, s32[128]{0:T(128)}, u32[]{:S(2)}) copy-start(s32[128]{0:T(128)} %param.14) | copy-start | bytes 1540
  7.7 0.7 %copy-start.8 = (s32[16,1]{0,1:T(1,128)S(1)}, s32[16,1]{0,1:T(1,128)}, u32[]{:S(2)}) copy-start(s32[16,1]{0,1:T(1,128)} %param.16) | copy-start | bytes 196

commit v3 on v2

--- a/solution.py
+++ b/solution.py
@@ -16,6 +16,7 @@
 PEER_MAX = 2
 MESH = pl.DeviceIdType.MESH
 LANES = 128
+VMEM_BYTES = 67043328
 
 
 def complex_times(left_factor, right_factor):
@@ -141,6 +142,8 @@
     serving_hbm,
     owner_hbm,
     table_hbm,
+    share_hbm,
+    rank_hbm,
     share_ref,
     rank_ref,
     coef_all,
@@ -178,6 +181,10 @@
     ring_recv_sem,
     local_sem,
     small_sem,
+    relay_send_sem,
+    relay_recv_sem,
+    share_sem,
+    rank_sem,
 ):
     stations, antennas, _, users, tones = guess.shape
     pieces = stations * antennas
@@ -281,11 +288,12 @@
         chosen = jnp.dot(pick[...], total, preferred_element_type=jnp.float32)
         coef_send[:, q] = chosen.astype(jnp.bfloat16).reshape(n, block, 2 * TAPS)
     coef_copies = []
+    mine_half = pl.ds(part * (pieces // 2), pieces // 2)
     for k in range(1, n):
         peer = lax.rem(me + k, n)
         copy = pltpu.make_async_remote_copy(
-            src_ref=coef_send.at[peer],
-            dst_ref=coef_all.at[me],
+            src_ref=coef_send.at[peer, mine_half],
+            dst_ref=coef_all.at[me, mine_half],
             send_sem=coef_send_sem.at[k],
             recv_sem=coef_recv_sem.at[n - k],
             device_id={"ap": peer},
@@ -444,9 +452,24 @@
             ).astype(jnp.int32)
 
 
-    for copy in coef_copies:
-        copy.wait_recv()
+    rank_copy = pltpu.make_async_copy(rank_ref, rank_hbm, rank_sem)
+    rank_copy.start()
+    relay_copies = []
+    for k in range(1, n):
+        coef_copies[n - k - 1].wait_recv()
+        origin = lax.rem(me + n - (n - k), n)
+        copy = pltpu.make_async_remote_copy(
+            src_ref=coef_all.at[origin, mine_half],
+            dst_ref=coef_all.at[origin, mine_half],
+            send_sem=relay_send_sem.at[k],
+            recv_sem=relay_recv_sem.at[k],
+            device_id={"sc": 1 - part},
+            device_id_type=MESH,
+        )
+        copy.start()
+        relay_copies.append(copy)
     own_coef.wait()
+    share_copies = []
 
     def combine(origin, c, source):
         base = c * width
@@ -492,21 +515,37 @@
             return carry
 
         lax.fori_loop(0, width // LANES, tile, 0)
+        place = (
+            pl.ds(c * (width // LANES), width // LANES),
+            pl.ds(origin * PEER_MAX, PEER_MAX),
+        )
+        copy = pltpu.make_async_copy(
+            share_ref.at[place], share_hbm.at[place], share_sem.at[len(share_copies)]
+        )
+        copy.start()
+        share_copies.append(copy)
 
     def drain(most):
         for _ in range(most):
             if ready:
                 combine(*ready.pop(0))
 
-    drain(2)
-    for late in range(chunks, chunks + steps + 1):
+    late_slots = range(chunks, chunks + steps)
+    for late in late_slots:
         for d in range(chunks):
             for direction in range(2):
                 if late - d > 0:
                     ring_start(d, direction, late - d)
-            drain(2)
+        if late == chunks:
+            for copy in relay_copies:
+                copy.wait_recv()
+        drain(-(-n * chunks // (steps + 1)))
     drain(len(ready))
-
+    rank_copy.wait()
+    for copy in share_copies:
+        copy.wait()
+    for copy in relay_copies:
+        copy.wait_send()
     for copy in half_copies:
         copy.wait_send()
     for copy in gain_copies:
@@ -518,35 +557,27 @@
 
 
 def second_kernel(n, rank_ref, share_ref, out_hbm, total, moved, out_sem):
-    tiles, _, rows, _ = share_ref.shape
+    _, _, rows, _ = share_ref.shape
     pairs = rows // (2 * CU)
-    height = CU * pairs * tiles * 2
+    tiles = pl.num_programs(0)
+    l = pl.program_id(0)
+    stride = moved.shape[0] // (OWN_MAX * CU)
+    height = CU * stride
     total[...] = jnp.zeros_like(total)
-    slots = [rank_ref[k, 0] for k in range(n * PEER_MAX)]
-
-    def tile(l, carry):
-        for k in range(n * PEER_MAX):
-            total[l, slots[k]] += share_ref[l, k]
-        return carry
-
-    lax.fori_loop(0, tiles, tile, 0)
-    copies = []
+    for k in range(n * PEER_MAX):
+        total[rank_ref[k, 0]] += share_ref[0, k]
     for r in range(OWN_MAX):
-
-        def move(l, carry, r=r):
-            for s in range(pairs):
-                for reim in range(2):
-                    moved[pl.ds(r * height + (s * tiles + l) * 2 + reim, CU, stride=pairs * tiles * 2), :] = (
-                        total[l, r, pl.ds((s * 2 + reim) * CU, CU), :]
-                    )
-            return carry
-
-        lax.fori_loop(0, tiles, move, 0)
-        part = pl.ds(r * height, height)
-        copy = pltpu.make_async_copy(moved.at[part], out_hbm.at[part], out_sem.at[r])
-        copy.start()
-        copies.append(copy)
-    for copy in copies:
+        for s in range(pairs):
+            for reim in range(2):
+                first = r * height + (s * tiles + l) * 2 + reim
+                moved[pl.ds(first, CU, stride=stride), :] = total[
+                    r, pl.ds((s * 2 + reim) * CU, CU), :
+                ]
+
+    @pl.when(l == tiles - 1)
+    def _():
+        copy = pltpu.make_async_copy(moved, out_hbm, out_sem)
+        copy.start()
         copy.wait()
 
 
@@ -625,8 +656,10 @@
             jax.ShapeDtypeStruct((n * PEER_MAX, LANES), jnp.int32),
         ),
         in_specs=[hbm] * 9,
-        out_specs=(vmem, vmem),
+        out_specs=(hbm, hbm),
         scratch_shapes=[
+            pltpu.VMEM((tiles, n * PEER_MAX, symbols * 2 * CU, LANES), f32),
+            pltpu.VMEM((n * PEER_MAX, LANES), jnp.int32),
             pltpu.VMEM((n, pieces, block, 2 * TAPS), bf16),
             pltpu.VMEM((n, chunks, antennas * 2 * rows, width), bf16),
             pltpu.VMEM((n, stations, block, LANES), f32),
@@ -662,9 +695,13 @@
             dma((2, chunks, steps)),
             dma,
             dma((7,)),
+            dma((n,)),
+            dma((n,)),
+            dma((n * chunks,)),
+            dma,
         ],
         compiler_params=pltpu.CompilerParams(
-            collective_id=0, has_side_effects=True, vmem_limit_bytes=40 * 1024 * 1024
+            collective_id=0, has_side_effects=True, vmem_limit_bytes=VMEM_BYTES
         ),
         name="smooth_solve_combine",
     )(
@@ -682,14 +719,20 @@
     placed = pl.pallas_call(
         functools.partial(second_kernel, n),
         out_shape=jax.ShapeDtypeStruct((lines, LANES), f32),
-        in_specs=[smem, vmem],
+        grid=(tiles,),
+        in_specs=[
+            smem,
+            pl.BlockSpec(
+                (1, n * PEER_MAX, symbols * 2 * CU, LANES), lambda l: (l, 0, 0, 0)
+            ),
+        ],
         out_specs=hbm,
         scratch_shapes=[
-            pltpu.VMEM((tiles, OWN_MAX, symbols * 2 * CU, LANES), f32),
+            pltpu.VMEM((OWN_MAX, symbols * 2 * CU, LANES), f32),
             pltpu.VMEM((lines, LANES), f32),
-            dma((OWN_MAX,)),
+            dma,
         ],
-        compiler_params=pltpu.CompilerParams(vmem_limit_bytes=16 * 1024 * 1024),
+        compiler_params=pltpu.CompilerParams(vmem_limit_bytes=VMEM_BYTES),
         name="place",
     )(rank, share)
     placed = placed.reshape(OWN_MAX, CU, symbols, tiles, 2, LANES)

time: 52.6 us -> 48.2 us (0.916)
  local copies, waits for them, and re-layouts: 8.31 us -> 0 us
  Pallas kernels: 44.1 us -> 47.9 us
    unnamed x18 -> x0, local copies, waits for them, and re-layouts: 8.31 us -> none
    pallas_call x1, Pallas kernels: 3.13 us -> 6.16 us  [local(): pl.pallas_call(functools.partial(second_kernel, n), out_shape=jax.ShapeDt...]
    pallas_call x1, Pallas kernels: 40.9 us -> 41.8 us  [local(): pl.pallas_call(functools.partial(first_kernel, n, chunks, ring_of), out_s...]
where the time goes in v3:
time: 48.2 us; the launch traced here: 47.9 us
  Pallas kernels  47.9 us (99%)
    pallas_call x1, Pallas kernels, local(): pl.pallas_call(functools.partial(first_kernel, n, chunks, ring_of), out_s...  41.8 us
    pallas_call x1, Pallas kernels, local(): pl.pallas_call(functools.partial(second_kernel, n), out_shape=jax.ShapeDt...  6.16 us

profile of v3, /device:TPU:0, one launch (start us, length us, event | category | flops | bytes accessed | tf_op | source)
XLA Modules:
  0.0 47.9 jit_solution(7418538115517457638)
XLA Ops:
  0.0 41.8 %smooth_solve_combine.1 = (f32[8,16,64,128]{3,2,1,0:T(8,128)}, s32[16,128]{1,0:T(8,128)}) custom-call(bf16[2,4,2,128,1024]{4,3,2,1,0:T(8,128)(2,1)} %guess_hbm.1, bf16[2,4,2,4,1024]{4,3,2,1,0:T(4,128)(2,1)} %received_hbm.1, f32[1,128]{1,0:T(1,128)} %bitcast.9, f32[1,2]{1,0:T(1,128)} %bitcast.10, f32[2,128]{1,0:T(2,128)} %gain_hbm.1, s32[1,128]{1,0:T(1,128)} %bitcast.11, ...), custom_call_target="tpu_custom_call" | custom-call | tf_op jit(solution)/shard_map/smooth_solve_combine/pallas_call | solution.py:652
  41.8 6.2 %place.1 = f32[2048,128]{1,0:T(8,128)} custom-call(s32[16,128]{1,0:T(8,128)} %get-tuple-element.7.rank_ref, f32[8,16,64,128]{3,2,1,0:T(8,128)} %get-tuple-element.8.share_ref), custom_call_target="tpu_custom_call" | custom-call | tf_op jit(solution)/shard_map/place/pallas_call | solution.py:719

commit v4 on v2

--- a/solution.py
+++ b/solution.py
@@ -16,6 +16,7 @@
 PEER_MAX = 2
 MESH = pl.DeviceIdType.MESH
 LANES = 128
+VMEM_BYTES = 67043328
 
 
 def complex_times(left_factor, right_factor):
@@ -178,6 +179,8 @@
     ring_recv_sem,
     local_sem,
     small_sem,
+    relay_send_sem,
+    relay_recv_sem,
 ):
     stations, antennas, _, users, tones = guess.shape
     pieces = stations * antennas
@@ -281,11 +284,12 @@
         chosen = jnp.dot(pick[...], total, preferred_element_type=jnp.float32)
         coef_send[:, q] = chosen.astype(jnp.bfloat16).reshape(n, block, 2 * TAPS)
     coef_copies = []
+    mine_half = pl.ds(part * (pieces // 2), pieces // 2)
     for k in range(1, n):
         peer = lax.rem(me + k, n)
         copy = pltpu.make_async_remote_copy(
-            src_ref=coef_send.at[peer],
-            dst_ref=coef_all.at[me],
+            src_ref=coef_send.at[peer, mine_half],
+            dst_ref=coef_all.at[me, mine_half],
             send_sem=coef_send_sem.at[k],
             recv_sem=coef_recv_sem.at[n - k],
             device_id={"ap": peer},
@@ -444,8 +448,20 @@
             ).astype(jnp.int32)
 
 
-    for copy in coef_copies:
-        copy.wait_recv()
+    relay_copies = []
+    for k in range(1, n):
+        coef_copies[n - k - 1].wait_recv()
+        origin = lax.rem(me + n - (n - k), n)
+        copy = pltpu.make_async_remote_copy(
+            src_ref=coef_all.at[origin, mine_half],
+            dst_ref=coef_all.at[origin, mine_half],
+            send_sem=relay_send_sem.at[k],
+            recv_sem=relay_recv_sem.at[k],
+            device_id={"sc": 1 - part},
+            device_id_type=MESH,
+        )
+        copy.start()
+        relay_copies.append(copy)
     own_coef.wait()
 
     def combine(origin, c, source):
@@ -498,15 +514,19 @@
             if ready:
                 combine(*ready.pop(0))
 
-    drain(2)
-    for late in range(chunks, chunks + steps + 1):
+    late_slots = range(chunks, chunks + steps)
+    for late in late_slots:
         for d in range(chunks):
             for direction in range(2):
                 if late - d > 0:
                     ring_start(d, direction, late - d)
-            drain(2)
+        if late == chunks:
+            for copy in relay_copies:
+                copy.wait_recv()
+        drain(-(-n * chunks // (steps + 1)))
     drain(len(ready))
-
+    for copy in relay_copies:
+        copy.wait_send()
     for copy in half_copies:
         copy.wait_send()
     for copy in gain_copies:
@@ -607,7 +627,7 @@
     pieces = stations * antennas
     block = PEER_MAX * CU
     rows = stations * symbols
-    chunks = 4
+    chunks = 2
     width = tones // chunks
     steps = n // 2
     table = jnp.asarray(delay_tables(parts, tones))
@@ -618,6 +638,7 @@
     bf16, f32 = jnp.bfloat16, jnp.float32
     hbm = pl.BlockSpec(memory_space=pltpu.HBM)
     tiles = tones // LANES
+    held = 4 * LANES * n * PEER_MAX * (tiles * symbols * 2 * CU + 1)
     share, rank = pl.pallas_call(
         functools.partial(first_kernel, n, chunks, ring_of),
         out_shape=(
@@ -662,9 +683,11 @@
             dma((2, chunks, steps)),
             dma,
             dma((7,)),
+            dma((n,)),
+            dma((n,)),
         ],
         compiler_params=pltpu.CompilerParams(
-            collective_id=0, has_side_effects=True, vmem_limit_bytes=40 * 1024 * 1024
+            collective_id=0, has_side_effects=True, vmem_limit_bytes=VMEM_BYTES - held
         ),
         name="smooth_solve_combine",
     )(

time: 52.6 us -> 44 us (0.84)
  local copies, waits for them, and re-layouts: 8.31 us -> 2.88 us
  Pallas kernels: 44.1 us -> 40.9 us
    unnamed x18 -> x4, local copies, waits for them, and re-layouts: 8.31 us -> 2.88 us
    pallas_call x1, Pallas kernels: 40.9 us -> 38.1 us  [local(): pl.pallas_call(functools.partial(first_kernel, n, chunks, ring_of), out_s...]
where the time goes in v4:
time: 44 us; the launch traced here: 43.8 us
  Pallas kernels  40.9 us (93%)
  local copies, waits for them, and re-layouts  2.88 us (7%)
    pallas_call x1, Pallas kernels, local(): pl.pallas_call(functools.partial(first_kernel, n, chunks, ring_of), out_s...  38.1 us
    unnamed x4, local copies, waits for them, and re-layouts  2.88 us
    pallas_call x1, Pallas kernels, local(): pl.pallas_call(functools.partial(second_kernel, n), out_shape=jax.ShapeDt...  2.84 us

profile of v4, /device:TPU:0, one launch (start us, length us, event | category | flops | bytes accessed | tf_op | source)
XLA Modules:
  0.0 43.8 jit_solution(7076269038939458767)
XLA Ops:
  0.0 38.1 %smooth_solve_combine.1 = (f32[8,16,64,128]{3,2,1,0:T(8,128)}, s32[16,128]{1,0:T(8,128)}) custom-call(bf16[2,4,2,128,1024]{4,3,2,1,0:T(8,128)(2,1)} %guess_hbm.1, bf16[2,4,2,4,1024]{4,3,2,1,0:T(4,128)(2,1)} %received_hbm.1, f32[1,128]{1,0:T(1,128)} %bitcast.9, f32[1,2]{1,0:T(1,128)} %bitcast.10, f32[2,128]{1,0:T(2,128)} %gain_hbm.1, s32[1,128]{1,0:T(1,128)} %bitcast.11, ...), custom_call_target="tpu_custom_call" | custom-call | tf_op jit(solution)/shard_map/smooth_solve_combine/pallas_call | solution.py:642
  38.1 0.0 copy-start
  38.1 2.2 %copy-done = f32[8,16,64,128]{3,2,1,0:T(8,128)S(1)} copy-done((f32[8,16,64,128]{3,2,1,0:T(8,128)S(1)}, f32[8,16,64,128]{3,2,1,0:T(8,128)}, u32[]{:S(2)}) %copy-start) | copy-done | bytes 4194328
  40.3 0.0 copy-start.1
  40.3 0.7 %copy-done.1 = s32[16,128]{1,0:T(8,128)S(1)} copy-done((s32[16,128]{1,0:T(8,128)S(1)}, s32[16,128]{1,0:T(8,128)}, u32[]{:S(2)}) %copy-start.1) | copy-done | bytes 8216
  41.0 2.8 %place.1 = f32[2048,128]{1,0:T(8,128)} custom-call(s32[16,128]{1,0:T(8,128)S(1)} %copy-done.1, f32[8,16,64,128]{3,2,1,0:T(8,128)S(1)} %copy-done), custom_call_target="tpu_custom_call" | custom-call | tf_op jit(solution)/shard_map/place/pallas_call | solution.py:705
Async XLA Ops:
  38.1 2.2 %copy-start = (f32[8,16,64,128]{3,2,1,0:T(8,128)S(1)}, f32[8,16,64,128]{3,2,1,0:T(8,128)}, u32[]{:S(2)}) copy-start(f32[8,16,64,128]{3,2,1,0:T(8,128)} %get-tuple-element.8.share_ref) | copy-start | bytes 12582916
  40.3 0.7 %copy-start.1 = (s32[16,128]{1,0:T(8,128)S(1)}, s32[16,128]{1,0:T(8,128)}, u32[]{:S(2)}) copy-start(s32[16,128]{1,0:T(8,128)} %get-tuple-element.7.rank_ref) | copy-start | bytes 24580
